TPU v7x, 768 devices: a whole 4x8x12 slice. The times are simulated.
768 devices in a mesh: group: 48 (over x, z), peer: 16 (over y, core).
Axes of the slice: x: 4, y: 8, z: 12, core: 2. Of those that a mesh axis runs over, the one named last changes fastest.
Arguments:
- points: bfloat16 [786432, 256], P(('group', 'peer')), may hold values from -6 to 6
- cotangent: bfloat16 [786432, 256], P(('group', 'peer')), may hold values from -6 to 6
- dest_code: int32 [6144], P(('group', 'peer')), may hold values from 0 to 15, as said below
- src_code: int32 [6144], P(('group', 'peer')), may hold values from 0 to 15, as said below
- w_qkv: bfloat16 [256, 768], replicated
- w_out: bfloat16 [256, 256], replicated, may hold values from -0.375 to 0.375
- norm_attn: float32 [256], replicated, may hold values from 0.25 to 1.75
- norm_mlp: float32 [256], replicated, may hold values from 0.25 to 1.75
- w_hidden: bfloat16 [256, 1024], replicated, may hold values from -0.375 to 0.375
- w_output: bfloat16 [1024, 256], replicated, may hold values from -0.1875 to 0.1875
Outputs:
- block_out: bfloat16 [786432, 256], P(('group', 'peer'))
- hidden_grad: float32 [256, 1024], P(None, 'peer')
- output_grad: float32 [1024, 256], P('peer')
Inputs may be any that keep to these rules, and one draw needn't show every extreme that they name: Within a device the entries are distinct; every device of a group receives exactly 8 blocks, and the sender's dest_code and the receiver's src_code name each moved block consistently. `src_code`: within a device the entries are distinct and name the blocks that dest_code sends to it.
All inputs are finite; a program needn't handle non-finite values.
Results may differ from a plain program's by a relative error of at most 0.014.
The roundings to bfloat16 on the way count: a program that leaves them out, or rounds other values in their place, can miss the bound.
Values may be sent and summed in bfloat16 or wider, within the bound.
A program may use at most 32 MiB of HBM per device.

v0:
```python
import jax
import jax.numpy as jnp
from jax import lax
from jax.sharding import PartitionSpec as P

D = 256
HEAD_DIM = 16
PATCH_BLOCKS = 4


def layer_norm(v):
    centre = v - jnp.mean(v, axis=-1, keepdims=True)
    spread = jnp.mean(centre * centre, axis=-1, keepdims=True)
    return centre * lax.rsqrt(spread + 1e-05)


def pack_blocks(arr, codes, slots, block_rows):
    width = arr.shape[1]
    pieces = arr.reshape(codes.shape[0], block_rows, width)
    return jnp.zeros((slots, block_rows, width), arr.dtype).at[codes].set(pieces)


def split_heads(mat, patches, patch, heads):
    return (
        mat.reshape(patches, patch, heads, HEAD_DIM)
        .transpose(0, 2, 1, 3)
        .reshape(patches * heads, patch, HEAD_DIM)
    )


def patch_attention(qkv, rows, patch):
    heads = D // HEAD_DIM
    patches = rows // patch
    query = split_heads(qkv[:, :D], patches, patch, heads)
    keys = split_heads(qkv[:, D : 2 * D], patches, patch, heads)
    values = split_heads(qkv[:, 2 * D :], patches, patch, heads)
    factor = 1.0 / jnp.sqrt(jnp.float32(HEAD_DIM))

    def one_head(triple):
        scores = (
            jnp.einsum("qe,ke->qk", triple[0], triple[1], preferred_element_type=jnp.float32)
            * factor
        )
        probs = jax.nn.softmax(scores, axis=-1).astype(jnp.bfloat16)
        return jnp.einsum("qk,ke->qe", probs, triple[2], preferred_element_type=jnp.float32).astype(
            jnp.bfloat16
        )

    mixed = lax.map(one_head, (query, keys, values), batch_size=4)
    return mixed.reshape(patches, heads, patch, HEAD_DIM).transpose(0, 2, 1, 3).reshape(rows, D)


def attend(feats, w_qkv, w_out, norm_attn, rows, patch):
    first = feats.astype(jnp.float32)
    normed = (layer_norm(first) * norm_attn).astype(jnp.bfloat16)
    qkv = jnp.dot(normed, w_qkv, preferred_element_type=jnp.float32).astype(jnp.bfloat16)
    att = patch_attention(qkv, rows, patch)
    return (first + jnp.dot(att, w_out, preferred_element_type=jnp.float32)).astype(jnp.bfloat16)


def mlp_terms(hidden_state, cot, norm_mlp, w_hidden, w_output, grad_scale):
    second = (layer_norm(hidden_state.astype(jnp.float32)) * norm_mlp).astype(jnp.bfloat16)
    pre = jnp.dot(second, w_hidden, preferred_element_type=jnp.float32)
    act, gelu_back = jax.vjp(lambda v: jax.nn.gelu(v, approximate=True), pre)
    act = act.astype(jnp.bfloat16)
    result = (
        hidden_state.astype(jnp.float32)
        + jnp.dot(act, w_output, preferred_element_type=jnp.float32)
    ).astype(jnp.bfloat16)
    out_term = jnp.einsum("rf,rd->fd", act, cot, preferred_element_type=jnp.float32) * grad_scale
    dact = jnp.einsum("rd,fd->rf", cot, w_output, preferred_element_type=jnp.float32)
    dpre = gelu_back(dact)[0].astype(jnp.bfloat16)
    hid_term = (
        jnp.einsum("rd,rf->df", second, dpre, preferred_element_type=jnp.float32) * grad_scale
    )
    return (result, hid_term, out_term)


def per_device(
    points, cotangent, dest_code, src_code, w_qkv, w_out, norm_attn, norm_mlp, w_hidden, w_output
):
    peers = lax.axis_size("peer")
    blocks_here = dest_code.shape[0]
    rows = points.shape[0]
    block_rows = rows // blocks_here
    slots_cap = (blocks_here + peers - 1) // peers
    slots = peers * slots_cap
    patch = PATCH_BLOCKS * block_rows
    total_points = rows * peers * lax.axis_size("group")
    grad_scale = 1.0 / jnp.sqrt(jnp.float32(total_points))
    point_buf = pack_blocks(points, dest_code, slots, block_rows)
    cot_buf = pack_blocks(cotangent, dest_code, slots, block_rows)
    got_points, got_cot = (
        lax.all_to_all(point_buf, "peer", split_axis=0, concat_axis=0, tiled=True),
        lax.all_to_all(cot_buf, "peer", split_axis=0, concat_axis=0, tiled=True),
    )
    feats = jnp.take(got_points, src_code, axis=0).reshape(rows, D)
    hidden_state = attend(feats, w_qkv, w_out, norm_attn, rows, patch)
    cot = jnp.take(got_cot, src_code, axis=0).reshape(rows, D)
    result, hid_term, out_term = mlp_terms(
        hidden_state, cot, norm_mlp, w_hidden, w_output, grad_scale
    )
    out_buf = pack_blocks(result, src_code, slots, block_rows)
    returned = lax.all_to_all(out_buf, "peer", split_axis=0, concat_axis=0, tiled=True)
    block_out = jnp.take(returned, dest_code, axis=0).reshape(rows, D)
    hid_full, out_full = lax.psum((hid_term, out_term), "group")
    hidden_grad, output_grad = (
        lax.psum_scatter(hid_full, "peer", scatter_dimension=1, tiled=True),
        lax.psum_scatter(out_full, "peer", scatter_dimension=0, tiled=True),
    )
    return (block_out, hidden_grad, output_grad)


def solution(mesh):
    return jax.shard_map(
        per_device,
        mesh=mesh,
        in_specs=(
            P(("group", "peer"), None),
            P(("group", "peer"), None),
            P(("group", "peer")),
            P(("group", "peer")),
            P(),
            P(),
            P(),
            P(),
            P(),
            P(),
        ),
        out_specs=(P(("group", "peer"), None), P(None, "peer"), P("peer", None)),
        check_vma=False,
    )
```

profile of v0, /device:TPU:1, one launch (start us, length us, event | category | flops | bytes accessed | tf_op | source)
XLA Modules:
  0.0 493.8 jit_solution(10944334038182807080)
XLA Ops:
  7.2 0.7 compare_select_fusion
  7.9 1.1 broadcast.95.clone.1
  9.0 2.7 scatter_fusion
  11.8 14.0 %all-to-all-start = ((bf16[16,128,256]{2,1,0:T(8,128)(2,1)}), bf16[16,128,256]{2,1,0:T(8,128)(2,1)S(1)}, u32[]{:S(2)}, u32[]{:S(2)}) async-start(bf16[16,128,256]{2,1,0:T(8,128)(2,1)} %scatter_fusion), calls=%async_computation | async-start | bytes 2097152 | tf_op jit(solution)/shard_map/all_to_all | solution.py:94
  25.7 1.1 broadcast.95.clone
  26.8 2.5 scatter_fusion.2
  29.3 24.4 %all-to-all-done = bf16[16,128,256]{2,1,0:T(8,128)(2,1)S(1)} async-done(((bf16[16,128,256]{2,1,0:T(8,128)(2,1)}), bf16[16,128,256]{2,1,0:T(8,128)(2,1)S(1)}, u32[]{:S(2)}, u32[]{:S(2)}) %all-to-all-start) | async-done | bytes 1048608 | tf_op jit(solution)/shard_map/all_to_all | solution.py:94
  53.7 3.6 all-to-all-start.2
  57.2 0.0 reduce-scatter.5.cloned.1.call-start
  57.3 0.6 gather_fusion
  57.9 0.3 convert_reduce_fusion.1
  58.2 0.5 multiply_reduce_fusion.1
  58.7 1.0 fusion.56
  59.7 0.6 convolution_convert_fusion
  60.3 1.1 fusion.77
  61.4 0.2 copy.25
  61.6 0.4 reshape.91
  62.0 0.9 copy.26
  62.8 1.2 copy.27
  64.1 0.4 reshape.92
  64.5 0.9 copy.28
  65.4 1.2 copy.23
  66.6 0.4 reshape.90
  67.0 0.1 copy.24
  67.1 59.9 %while.10 = (s32[]{:T(128)}, bf16[8,4,512,16]{2,3,1,0:T(8,128)(2,1)}, bf16[8,4,512,16]{2,3,1,0:T(8,128)(2,1)S(1)}, bf16[8,4,512,16]{2,3,1,0:T(8,128)(2,1)}, bf16[8,4,512,16]{2,3,1,0:T(8,128)(2,1)}, /*index=5*/s32[]{:T(128)}) while((s32[]{:T(128)}, bf16[8,4,512,16]{2,3,1,0:T(8,128)(2,1)}, bf16[8,4,512,16]{2,3,1,0:T(8,128)(2,1)S(1)}, ...), condition=%wide.region_6.8_spmd, body=%wide.region_3.7_spmd.sunk | while | flops 72385024 | bytes 8669253 | solution.py:49
  67.1 4.2 fusion.95
  71.3 3.3 fusion.96
  74.6 4.2 fusion.95
  78.8 3.3 fusion.96
  82.1 4.2 fusion.95
  86.3 3.3 fusion.96
  89.6 4.2 fusion.95
  93.8 3.3 fusion.96
  97.0 4.2 fusion.95
  101.3 3.3 fusion.96
  104.5 4.2 fusion.95
  108.7 3.3 fusion.96
  112.0 4.2 fusion.95
  116.2 3.3 fusion.96
  119.5 4.2 fusion.95
  123.7 3.3 fusion.96
  126.9 1.6 copy.29
  128.6 0.1 copy.31
  128.7 0.6 gather_fusion.2
  129.2 0.2 broadcast_select_fusion.1
  129.4 0.5 convert_reduce_fusion
  129.9 0.4 fusion.51
  130.3 0.8 fusion.65
  131.1 1.9 copy-done.1
  133.0 2.5 convolution_multiply_fusion
  135.5 0.2 reduce-scatter.3.cloned.1.call-start
  135.8 6.9 %fusion.46 = f32[256,1024]{0,1:T(8,128)} fusion(f32[1024,1024]{1,0:T(8,128)} %copy-done.1, bf16[1024,256]{1,0:T(8,128)(2,1)S(1)} %bitcast.99, bf16[1024,256]{1,0:T(8,128)(2,1)S(1)} %copy-done.6, bf16[1024,256]{1,0:T(8,128)(2,1)S(1)} %get-tuple-element.54, f32[256]{0:T(256)S(1)} %copy-done.5, f32[1024]{0:T(1024)S(1)} %add_rsqrt_fusion, ...), kind=kOutput, calls=%fused_computation.49 | convolution fusion | flops 1096286208 | bytes 6824960 | tf_op jit(solution)/shard_map/rd,rf->df/dot_general | solution.py:74
  142.6 3.7 fusion.47
  146.3 1.1 broadcast.95
  147.4 2.5 scatter_fusion.1
  149.9 7.2 %all-to-all-start.1 = ((bf16[16,128,256]{2,1,0:T(8,128)(2,1)}), bf16[16,128,256]{2,1,0:T(8,128)(2,1)S(1)}, u32[]{:S(2)}, u32[]{:S(2)}) async-start(bf16[16,128,256]{2,1,0:T(8,128)(2,1)} %scatter_fusion.1), calls=%async_computation.1 | async-start | bytes 2097152 | tf_op jit(solution)/shard_map/all_to_all | solution.py:104
  157.2 29.6 %all-to-all-done.1 = bf16[16,128,256]{2,1,0:T(8,128)(2,1)S(1)} async-done(((bf16[16,128,256]{2,1,0:T(8,128)(2,1)}), bf16[16,128,256]{2,1,0:T(8,128)(2,1)S(1)}, u32[]{:S(2)}, u32[]{:S(2)}) %all-to-all-start.1) | async-done | bytes 1048608 | tf_op jit(solution)/shard_map/all_to_all | solution.py:104
  186.8 0.6 gather_fusion.1
  187.4 18.2 %reduce-scatter.5.cloned.1.call-done = f32[64,256]{1,0:T(8,128)} async-done(((f32[1024,256]{1,0:T(8,128)}), f32[64,256]{1,0:T(8,128)}) %reduce-scatter.5.cloned.1.call-update) | async-done | bytes 65552 | tf_op jit(solution)/shard_map/reduce_scatter | solution.py:109
  205.5 68.5 %reduce-scatter.3.cloned.1.call-done = f32[256,64]{0,1:T(8,128)} async-done(((f32[256,1024]{0,1:T(8,128)}), f32[256,64]{0,1:T(8,128)}) %reduce-scatter.3.cloned.1.call-update) | async-done | bytes 65552 | tf_op jit(solution)/shard_map/reduce_scatter | solution.py:108
  274.1 0.9 broadcast_select_fusion
  275.0 209.4 %all-reduce.3.cloned.1.call-done = (f32[256,64]{0,1:T(8,128)}, f32[64,256]{1,0:T(8,128)}) async-done(((f32[256,64]{0,1:T(8,128)}, f32[64,256]{1,0:T(8,128)}), (f32[256,64]{0,1:T(8,128)}, f32[64,256]{1,0:T(8,128)})) %all-reduce.3.cloned.1.call-update) | async-done | bytes 131088 | tf_op jit(solution)/shard_map/psum | solution.py:106
  484.4 1.5 copy.46
  485.8 1.5 copy.47
  (32 shorter events, 0.2 us)
Async XLA Ops:
  7.2 123.1 %copy-start = (bf16[256,1024]{1,0:T(8,128)(2,1)S(1)}, bf16[256,1024]{1,0:T(8,128)(2,1)}, u32[]{:S(2)}) copy-start(bf16[256,1024]{1,0:T(8,128)(2,1)} %param.22) | copy-start | bytes 1572868
  7.2 19.6 %copy-start.2 = (bf16[1024,256]{1,0:T(8,128)(2,1)S(1)}, bf16[1024,256]{1,0:T(8,128)(2,1)}, u32[]{:S(2)}) copy-start(bf16[1024,256]{1,0:T(8,128)(2,1)} %param.15) | copy-start | bytes 1572868
  7.2 22.1 %copy-start.7 = (s32[8]{0:T(128)S(1)}, s32[8]{0:T(128)}, u32[]{:S(2)}) copy-start(s32[8]{0:T(128)} %param.17) | copy-start | bytes 100
  11.8 41.9 %all-to-all-start = ((bf16[16,128,256]{2,1,0:T(8,128)(2,1)}), bf16[16,128,256]{2,1,0:T(8,128)(2,1)S(1)}, u32[]{:S(2)}, u32[]{:S(2)}) async-start(bf16[16,128,256]{2,1,0:T(8,128)(2,1)} %scatter_fusion), calls=%async_computation | async-start | bytes 2097152 | tf_op jit(solution)/shard_map/all_to_all | solution.py:94
  25.7 34.0 %copy-start.3 = (bf16[256,768]{1,0:T(8,128)(2,1)S(1)}, bf16[256,768]{1,0:T(8,128)(2,1)}, u32[]{:S(2)}) copy-start(bf16[256,768]{1,0:T(8,128)(2,1)} %param.18) | copy-start | bytes 1179652
  53.7 75.0 %all-to-all-start.2 = ((bf16[16,128,256]{2,1,0:T(8,128)(2,1)}), bf16[16,128,256]{2,1,0:T(8,128)(2,1)S(1)}, u32[]{:S(2)}, u32[]{:S(2)}) async-start(bf16[16,128,256]{2,1,0:T(8,128)(2,1)} %scatter_fusion.2), calls=%async_computation.2 | async-start | bytes 2097152 | tf_op jit(solution)/shard_map/all_to_all | solution.py:95
  57.2 148.3 %reduce-scatter.5.cloned.1.call-start = ((), (), s32[]{:S(2)}) async-start(), calls=%async_computation.6 | async-start | bytes 1114112 | tf_op jit(solution)/shard_map/reduce_scatter | solution.py:109
  126.9 2.5 copy-start.4
  126.9 3.4 copy-start.5
  131.1 1.9 copy-start.1
  133.0 2.8 copy-start.6
  135.5 138.5 %reduce-scatter.3.cloned.1.call-start = ((), (), s32[]{:S(2)}) async-start(), calls=%async_computation.5 | async-start | bytes 1114112 | tf_op jit(solution)/shard_map/reduce_scatter | solution.py:108
  146.3 10.8 %copy-start.8 = (s32[8]{0:T(128)S(1)}, s32[8]{0:T(128)}, u32[]{:S(2)}) copy-start(s32[8]{0:T(128)} %param.16) | copy-start | bytes 100
  149.9 36.8 %all-to-all-start.1 = ((bf16[16,128,256]{2,1,0:T(8,128)(2,1)}), bf16[16,128,256]{2,1,0:T(8,128)(2,1)S(1)}, u32[]{:S(2)}, u32[]{:S(2)}) async-start(bf16[16,128,256]{2,1,0:T(8,128)(2,1)} %scatter_fusion.1), calls=%async_computation.1 | async-start | bytes 2097152 | tf_op jit(solution)/shard_map/all_to_all | solution.py:104
  157.1 327.2 %all-reduce.3.cloned.1.call-start = ((), (), s32[]{:S(2)}) async-start(), calls=%async_computation.7 | async-start | bytes 262144 | tf_op jit(solution)/shard_map/psum | solution.py:106
Sparse Core Ops, SparseCore 0:
  135.6 69.8 reduce-scatter.4
  208.9 65.0 reduce-scatter.2
  277.6 206.6 all-reduce.2
where the time goes:
time: 501 us; the launch traced here: 494 us
  waiting for transfers between devices  350 us (70%)
  matrix products  74.7 us (15%)
  local copies, waits for them, and re-layouts  26 us (5%)
  starting transfers between devices  25 us (5%)
  between operations  14 us (3%)
    psum x1, waiting for transfers between devices, per_device(): hid_full, out_full = lax.psum((hid_term, out_term), 'group')  209 us
    reduce_scatter x1, waiting for transfers between devices, per_device(): lax.psum_scatter(hid_full, 'peer', scatter_dimension=1, tiled=True)  68.5 us
    sub x8, matrix products, one_head(): probs = jax.nn.softmax(scores, axis=-1).astype(jnp.bfloat16)  33.8 us
    all_to_all x1, waiting for transfers between devices, per_device(): lax.all_to_all(out_buf, 'peer', split_axis=0, concat_axis=0, tiled=True)  29.6 us
    dot_general x8, matrix products, one_head(): jnp.einsum('qk,ke->qe', probs, triple[2], preferred_element_type=jnp.floa...  26 us
    all_to_all x1, waiting for transfers between devices, per_device(): lax.all_to_all(point_buf, 'peer', split_axis=0, concat_axis=0, tiled=True)  24.4 us
    reduce_scatter x1, waiting for transfers between devices, per_device(): lax.psum_scatter(out_full, 'peer', scatter_dimension=0, tiled=True)  18.2 us
    all_to_all x1, starting transfers between devices, per_device(): lax.all_to_all(point_buf, 'peer', split_axis=0, concat_axis=0, tiled=True)  14 us
  transfers between devices with their start and end apart: 6, of which 5 were waited for; matrix products, arithmetic and copies ran while one was open for 18% of the time, Pallas kernels for 0%

commit v1 on v0

v1 whole, which is shorter than its diff:
```python
import jax
import jax.numpy as jnp
from jax import lax
from jax.sharding import PartitionSpec as P

D = 256
HEAD_DIM = 16
PATCH_BLOCKS = 4


def layer_norm(v):
    centre = v - jnp.mean(v, axis=-1, keepdims=True)
    spread = jnp.mean(centre * centre, axis=-1, keepdims=True)
    return centre * lax.rsqrt(spread + 1e-05)


def pack_blocks(arr, codes, slots, block_rows):
    width = arr.shape[1]
    pieces = arr.reshape(codes.shape[0], block_rows, width)
    return jnp.zeros((slots, block_rows, width), arr.dtype).at[codes].set(pieces)


def split_heads(mat, patches, patch, heads):
    return (
        mat.reshape(patches, patch, heads, HEAD_DIM)
        .transpose(0, 2, 1, 3)
        .reshape(patches * heads, patch, HEAD_DIM)
    )


def patch_attention(qkv, rows, patch):
    heads = D // HEAD_DIM
    patches = rows // patch
    query = split_heads(qkv[:, :D], patches, patch, heads)
    keys = split_heads(qkv[:, D : 2 * D], patches, patch, heads)
    values = split_heads(qkv[:, 2 * D :], patches, patch, heads)
    factor = 1.0 / jnp.sqrt(jnp.float32(HEAD_DIM))

    def one_head(triple):
        scores = (
            jnp.einsum("qe,ke->qk", triple[0], triple[1], preferred_element_type=jnp.float32)
            * factor
        )
        probs = jax.nn.softmax(scores, axis=-1).astype(jnp.bfloat16)
        return jnp.einsum("qk,ke->qe", probs, triple[2], preferred_element_type=jnp.float32).astype(
            jnp.bfloat16
        )

    mixed = lax.map(one_head, (query, keys, values), batch_size=4)
    return mixed.reshape(patches, heads, patch, HEAD_DIM).transpose(0, 2, 1, 3).reshape(rows, D)


def attend(feats, w_qkv, norm_attn, rows, patch):
    normed = (layer_norm(feats.astype(jnp.float32)) * norm_attn).astype(jnp.bfloat16)
    qkv = jnp.dot(normed, w_qkv, preferred_element_type=jnp.float32).astype(jnp.bfloat16)
    return patch_attention(qkv, rows, patch)


def mlp_terms(hidden_state, cot, norm_mlp, w_hidden, w_output):
    second = (layer_norm(hidden_state.astype(jnp.float32)) * norm_mlp).astype(jnp.bfloat16)
    pre = jnp.dot(second, w_hidden, preferred_element_type=jnp.float32)
    act, gelu_back = jax.vjp(lambda v: jax.nn.gelu(v, approximate=True), pre)
    act = act.astype(jnp.bfloat16)
    result = (
        hidden_state.astype(jnp.float32)
        + jnp.dot(act, w_output, preferred_element_type=jnp.float32)
    ).astype(jnp.bfloat16)
    out_term = jnp.einsum("rf,rd->fd", act, cot, preferred_element_type=jnp.float32)
    dact = jnp.einsum("rd,fd->rf", cot, w_output, preferred_element_type=jnp.float32)
    dpre = gelu_back(dact)[0].astype(jnp.bfloat16)
    hid_term = jnp.einsum("rf,rd->fd", dpre, second, preferred_element_type=jnp.float32)
    return (result, hid_term, out_term)


def redeal(blocks, send_codes, take_codes, slots, block_rows):
    buf = pack_blocks(blocks, send_codes, slots, block_rows)
    got = lax.all_to_all(buf, "peer", split_axis=0, concat_axis=0, tiled=True)
    return jnp.take(got, take_codes, axis=0).reshape(blocks.shape)


def swap(pieces, axis):
    return lax.all_to_all(pieces, axis, split_axis=0, concat_axis=0, tiled=True)


def sum_grads(hid_term, out_term, peers, groups, scale):
    units = hid_term.shape[0] // peers
    both = jnp.concatenate(
        [hid_term.reshape(peers, units, D), out_term.reshape(peers, units, D)], axis=1
    ).astype(jnp.bfloat16)
    share = jnp.sum(swap(both, "peer").astype(jnp.float32), axis=0) * scale
    flat = share.reshape(-1, 8, 128)
    pieces = flat.shape[0]
    per = -(-pieces // groups)
    padded = jnp.pad(flat, ((0, per * groups - pieces), (0, 0), (0, 0)))
    mine = jnp.sum(
        swap(padded, "group").reshape(groups, per, 8, 128), axis=0
    )
    everyone = jnp.broadcast_to(mine[None], (groups, per, 8, 128)).reshape(groups * per, 8, 128)
    total = swap(everyone, "group")[:pieces].reshape(2 * units, D)
    return total[:units].T, total[units:]


def per_device(
    points, cotangent, dest_code, src_code, w_qkv, w_out, norm_attn, norm_mlp, w_hidden, w_output
):
    peers = lax.axis_size("peer")
    groups = lax.axis_size("group")
    blocks_here = dest_code.shape[0]
    rows = points.shape[0]
    block_rows = rows // blocks_here
    slots = peers * ((blocks_here + peers - 1) // peers)
    patch = PATCH_BLOCKS * block_rows
    grad_scale = 1.0 / jnp.sqrt(jnp.float32(rows * peers * groups))
    feats = redeal(points, dest_code, src_code, slots, block_rows)
    att = attend(feats, w_qkv, norm_attn, rows, patch)
    att = redeal(att, src_code, dest_code, slots, block_rows)
    hidden_state = (
        points.astype(jnp.float32) + jnp.dot(att, w_out, preferred_element_type=jnp.float32)
    ).astype(jnp.bfloat16)
    result, hid_term, out_term = mlp_terms(hidden_state, cotangent, norm_mlp, w_hidden, w_output)
    hidden_grad, output_grad = sum_grads(hid_term, out_term, peers, groups, grad_scale)
    return (result, hidden_grad, output_grad)


def solution(mesh):
    return jax.shard_map(
        per_device,
        mesh=mesh,
        in_specs=(
            P(("group", "peer"), None),
            P(("group", "peer"), None),
            P(("group", "peer")),
            P(("group", "peer")),
            P(),
            P(),
            P(),
            P(),
            P(),
            P(),
        ),
        out_specs=(P(("group", "peer"), None), P(None, "peer"), P("peer", None)),
        check_vma=False,
    )
```

time: 501 us -> 238 us (0.48); the launches traced: 494 us -> 236 us
  waiting for transfers between devices: 350 us -> 66.5 us
  blocking collectives: 0 us -> 59.7 us
  between operations: 14 us -> 1.02 us
  local copies, waits for them, and re-layouts: 26 us -> 16.5 us
  matrix products: 74.7 us -> 67.6 us
    psum x1 -> x0, waiting for transfers between devices: 209 us -> none  [per_device(): hid_full, out_full = lax.psum((hid_term, out_term), 'group')]
    reduce_scatter x2 -> x0, waiting for transfers between devices: 86.7 us -> none  [the longest x1 68.5 us: per_device(): lax.psum_scatter(hid_full, 'peer', scatter_dimension=1, tiled=True)]
    all_to_all x0 -> x2, blocking collectives: none -> 59.7 us  [swap(): return lax.all_to_all(pieces, axis, split_axis=0, concat_axis=0, tiled=True)]
    all_to_all x3, waiting for transfers between devices: 54 us -> 66.5 us  [the longest x2 55.4 us: redeal(): got = lax.all_to_all(buf, 'peer', split_axis=0, concat_axis=0, tiled=True)]
    dot_general x8, matrix products: 26 us -> 20.6 us  [one_head(): jnp.einsum('qk,ke->qe', probs, triple[2], preferred_element_type=jnp.floa...]
  transfers between devices with their start and end apart: 6 -> 3, of which waited for: 5 -> 3; matrix products, arithmetic and copies ran while one was open for 18% -> 2% of each run, Pallas kernels for 0% -> 0%
where the time goes in v1:
time: 238 us; the launch traced here: 236 us
  matrix products  67.6 us (28%)
  waiting for transfers between devices  66.5 us (28%)
  blocking collectives  59.7 us (25%)
  starting transfers between devices  22.5 us (9%)
  local copies, waits for them, and re-layouts  16.5 us (7%)
  other arithmetic  2.55 us (1%)
    all_to_all x2, blocking collectives, swap(): return lax.all_to_all(pieces, axis, split_axis=0, concat_axis=0, tiled=True)  59.7 us
    all_to_all x2, waiting for transfers between devices, redeal(): got = lax.all_to_all(buf, 'peer', split_axis=0, concat_axis=0, tiled=True)  55.4 us
    sub x8, matrix products, one_head(): probs = jax.nn.softmax(scores, axis=-1).astype(jnp.bfloat16)  33.9 us
    dot_general x8, matrix products, one_head(): jnp.einsum('qk,ke->qe', probs, triple[2], preferred_element_type=jnp.floa...  20.6 us
    all_to_all x2, starting transfers between devices, redeal(): got = lax.all_to_all(buf, 'peer', split_axis=0, concat_axis=0, tiled=True)  17.7 us
    all_to_all x1, waiting for transfers between devices, swap(): return lax.all_to_all(pieces, axis, split_axis=0, concat_axis=0, tiled=True)  11.2 us
    dot_general x1, matrix products, mlp_terms(): jnp.einsum('rf,rd->fd', dpre, second, preferred_element_type=jnp.float32)  5.56 us
    scatter x2, local copies, waits for them, and re-layouts, pack_blocks(): jnp.zeros((slots, block_rows, width), arr.dtype).at[codes].set(pieces)  5.21 us
  transfers between devices with their start and end apart: 3, of which 3 were waited for; matrix products, arithmetic and copies ran while one was open for 2% of the time, Pallas kernels for 0%

profile of v1, /device:TPU:1, one launch (start us, length us, event | category | flops | bytes accessed | tf_op | source)
XLA Modules:
  0.0 236.4 jit_solution(10838602301124220282)
XLA Ops:
  0.7 0.7 compare_select_fusion
  1.4 1.1 broadcast.103.clone
  2.5 2.7 %scatter_fusion = bf16[16,128,256]{2,1,0:T(8,128)(2,1)} fusion(bf16[16,128,256]{2,1,0:T(8,128)(2,1)} %broadcast.103.clone, s32[8]{0:T(128)S(1)} %compare_select_fusion, bf16[8,128,256]{2,1,0:T(8,128)(2,1)} %bitcast.85), kind=kCustom, calls=%fused_computation.2 | custom fusion | bytes 1572896 | tf_op jit(solution)/shard_map/scatter | solution.py:20
  5.2 13.9 %all-to-all-start = ((bf16[16,128,256]{2,1,0:T(8,128)(2,1)}), bf16[16,128,256]{2,1,0:T(8,128)(2,1)S(1)}, u32[]{:S(2)}, u32[]{:S(2)}) async-start(bf16[16,128,256]{2,1,0:T(8,128)(2,1)} %scatter_fusion), calls=%async_computation | async-start | bytes 2097152 | tf_op jit(solution)/shard_map/all_to_all | solution.py:77
  19.2 27.9 %all-to-all-done = bf16[16,128,256]{2,1,0:T(8,128)(2,1)S(1)} async-done(((bf16[16,128,256]{2,1,0:T(8,128)(2,1)}), bf16[16,128,256]{2,1,0:T(8,128)(2,1)S(1)}, u32[]{:S(2)}, u32[]{:S(2)}) %all-to-all-start) | async-done | bytes 1048608 | tf_op jit(solution)/shard_map/all_to_all | solution.py:77
  47.1 0.6 gather_fusion
  47.7 0.3 fusion.67
  48.0 0.1 select_convert_fusion
  48.1 0.5 multiply_reduce_fusion.1
  48.6 0.3 fusion.56
  49.0 0.6 convolution_convert_fusion
  49.6 0.1 fusion.77
  49.7 0.2 copy.44
  49.9 0.4 reshape.103
  50.3 0.9 copy.45
  51.1 0.2 copy.46
  51.4 0.4 reshape.104
  51.7 0.1 copy.47
  51.8 0.2 copy.42
  52.0 0.4 reshape.102
  52.4 0.1 copy.43
  52.5 54.5 %while.10 = (s32[]{:T(128)}, bf16[8,4,512,16]{2,3,1,0:T(8,128)(2,1)S(1)}, bf16[8,4,512,16]{2,3,1,0:T(8,128)(2,1)S(1)}, bf16[8,4,512,16]{2,3,1,0:T(8,128)(2,1)}, bf16[8,4,512,16]{2,3,1,0:T(8,128)(2,1)S(1)}, /*index=5*/s32[]{:T(128)}) while((s32[]{:T(128)}, bf16[8,4,512,16]{2,3,1,0:T(8,128)(2,1)S(1)}, bf16[8,4,512,16]{2,3,1,0:T(8,128)(2,1)S(1)}, ...), condition=%wide.region_6.8_spmd, body=%wide.region_3.7_spmd.sunk | while | flops 72385024 | bytes 8669253 | solution.py:49
  52.5 4.2 %fusion.98 = (f32[4,512]{1,0:T(4,128)S(1)}, f32[4,512,512]{1,2,0:T(8,128)}) fusion(bf16[8,4,512,16]{2,3,1,0:T(8,128)(2,1)} %get-tuple-element.117, s32[]{:T(128)} %get-tuple-element.108, bf16[8,4,512,16]{2,3,1,0:T(8,128)(2,1)S(1)} %get-tuple-element.116), kind=kOutput, calls=%fused_computation.85.clone.1 | convolution fusion | flops 36700672 | bytes 4334592 | tf_op jit(solution)/shard_map/while/body/eval_jaxpr/vmap()/sub | solution.py:44
  56.7 2.6 %fusion.99 = bf16[8,4,512,16]{2,3,1,0:T(8,128)(2,1)S(1)} fusion(bf16[8,4,512,16]{2,3,1,0:T(8,128)(2,1)S(1)} %get-tuple-element.109, s32[]{:T(128)} %get-tuple-element.108, f32[4,512,512]{1,2,0:T(8,128)} %get-tuple-element.100, f32[4,512]{1,0:T(4,128)S(1)} %get-tuple-element.101, bf16[8,4,512,16]{2,3,1,0:T(8,128)(2,1)S(1)} %get-tuple-element.118), kind=kOutput, calls=%fused_computation.13.clone.1 | convolution fusion | flops 35684352 | bytes 4334592 | tf_op jit(solution)/shard_map/while/body/eval_jaxpr/vmap(qk,ke->qe)/dot_general | solution.py:45
  59.3 4.2 %fusion.98 = (f32[4,512]{1,0:T(4,128)S(1)}, f32[4,512,512]{1,2,0:T(8,128)}) fusion(bf16[8,4,512,16]{2,3,1,0:T(8,128)(2,1)} %get-tuple-element.117, s32[]{:T(128)} %get-tuple-element.108, bf16[8,4,512,16]{2,3,1,0:T(8,128)(2,1)S(1)} %get-tuple-element.116), kind=kOutput, calls=%fused_computation.85.clone.1 | convolution fusion | flops 36700672 | bytes 4334592 | tf_op jit(solution)/shard_map/while/body/eval_jaxpr/vmap()/sub | solution.py:44
  63.5 2.6 %fusion.99 = bf16[8,4,512,16]{2,3,1,0:T(8,128)(2,1)S(1)} fusion(bf16[8,4,512,16]{2,3,1,0:T(8,128)(2,1)S(1)} %get-tuple-element.109, s32[]{:T(128)} %get-tuple-element.108, f32[4,512,512]{1,2,0:T(8,128)} %get-tuple-element.100, f32[4,512]{1,0:T(4,128)S(1)} %get-tuple-element.101, bf16[8,4,512,16]{2,3,1,0:T(8,128)(2,1)S(1)} %get-tuple-element.118), kind=kOutput, calls=%fused_computation.13.clone.1 | convolution fusion | flops 35684352 | bytes 4334592 | tf_op jit(solution)/shard_map/while/body/eval_jaxpr/vmap(qk,ke->qe)/dot_general | solution.py:45
  66.1 4.2 %fusion.98 = (f32[4,512]{1,0:T(4,128)S(1)}, f32[4,512,512]{1,2,0:T(8,128)}) fusion(bf16[8,4,512,16]{2,3,1,0:T(8,128)(2,1)} %get-tuple-element.117, s32[]{:T(128)} %get-tuple-element.108, bf16[8,4,512,16]{2,3,1,0:T(8,128)(2,1)S(1)} %get-tuple-element.116), kind=kOutput, calls=%fused_computation.85.clone.1 | convolution fusion | flops 36700672 | bytes 4334592 | tf_op jit(solution)/shard_map/while/body/eval_jaxpr/vmap()/sub | solution.py:44
  70.4 2.6 %fusion.99 = bf16[8,4,512,16]{2,3,1,0:T(8,128)(2,1)S(1)} fusion(bf16[8,4,512,16]{2,3,1,0:T(8,128)(2,1)S(1)} %get-tuple-element.109, s32[]{:T(128)} %get-tuple-element.108, f32[4,512,512]{1,2,0:T(8,128)} %get-tuple-element.100, f32[4,512]{1,0:T(4,128)S(1)} %get-tuple-element.101, bf16[8,4,512,16]{2,3,1,0:T(8,128)(2,1)S(1)} %get-tuple-element.118), kind=kOutput, calls=%fused_computation.13.clone.1 | convolution fusion | flops 35684352 | bytes 4334592 | tf_op jit(solution)/shard_map/while/body/eval_jaxpr/vmap(qk,ke->qe)/dot_general | solution.py:45
  72.9 4.2 %fusion.98 = (f32[4,512]{1,0:T(4,128)S(1)}, f32[4,512,512]{1,2,0:T(8,128)}) fusion(bf16[8,4,512,16]{2,3,1,0:T(8,128)(2,1)} %get-tuple-element.117, s32[]{:T(128)} %get-tuple-element.108, bf16[8,4,512,16]{2,3,1,0:T(8,128)(2,1)S(1)} %get-tuple-element.116), kind=kOutput, calls=%fused_computation.85.clone.1 | convolution fusion | flops 36700672 | bytes 4334592 | tf_op jit(solution)/shard_map/while/body/eval_jaxpr/vmap()/sub | solution.py:44
  77.2 2.6 %fusion.99 = bf16[8,4,512,16]{2,3,1,0:T(8,128)(2,1)S(1)} fusion(bf16[8,4,512,16]{2,3,1,0:T(8,128)(2,1)S(1)} %get-tuple-element.109, s32[]{:T(128)} %get-tuple-element.108, f32[4,512,512]{1,2,0:T(8,128)} %get-tuple-element.100, f32[4,512]{1,0:T(4,128)S(1)} %get-tuple-element.101, bf16[8,4,512,16]{2,3,1,0:T(8,128)(2,1)S(1)} %get-tuple-element.118), kind=kOutput, calls=%fused_computation.13.clone.1 | convolution fusion | flops 35684352 | bytes 4334592 | tf_op jit(solution)/shard_map/while/body/eval_jaxpr/vmap(qk,ke->qe)/dot_general | solution.py:45
  79.8 4.2 %fusion.98 = (f32[4,512]{1,0:T(4,128)S(1)}, f32[4,512,512]{1,2,0:T(8,128)}) fusion(bf16[8,4,512,16]{2,3,1,0:T(8,128)(2,1)} %get-tuple-element.117, s32[]{:T(128)} %get-tuple-element.108, bf16[8,4,512,16]{2,3,1,0:T(8,128)(2,1)S(1)} %get-tuple-element.116), kind=kOutput, calls=%fused_computation.85.clone.1 | convolution fusion | flops 36700672 | bytes 4334592 | tf_op jit(solution)/shard_map/while/body/eval_jaxpr/vmap()/sub | solution.py:44
  84.0 2.6 %fusion.99 = bf16[8,4,512,16]{2,3,1,0:T(8,128)(2,1)S(1)} fusion(bf16[8,4,512,16]{2,3,1,0:T(8,128)(2,1)S(1)} %get-tuple-element.109, s32[]{:T(128)} %get-tuple-element.108, f32[4,512,512]{1,2,0:T(8,128)} %get-tuple-element.100, f32[4,512]{1,0:T(4,128)S(1)} %get-tuple-element.101, bf16[8,4,512,16]{2,3,1,0:T(8,128)(2,1)S(1)} %get-tuple-element.118), kind=kOutput, calls=%fused_computation.13.clone.1 | convolution fusion | flops 35684352 | bytes 4334592 | tf_op jit(solution)/shard_map/while/body/eval_jaxpr/vmap(qk,ke->qe)/dot_general | solution.py:45
  86.6 4.2 %fusion.98 = (f32[4,512]{1,0:T(4,128)S(1)}, f32[4,512,512]{1,2,0:T(8,128)}) fusion(bf16[8,4,512,16]{2,3,1,0:T(8,128)(2,1)} %get-tuple-element.117, s32[]{:T(128)} %get-tuple-element.108, bf16[8,4,512,16]{2,3,1,0:T(8,128)(2,1)S(1)} %get-tuple-element.116), kind=kOutput, calls=%fused_computation.85.clone.1 | convolution fusion | flops 36700672 | bytes 4334592 | tf_op jit(solution)/shard_map/while/body/eval_jaxpr/vmap()/sub | solution.py:44
  90.8 2.6 %fusion.99 = bf16[8,4,512,16]{2,3,1,0:T(8,128)(2,1)S(1)} fusion(bf16[8,4,512,16]{2,3,1,0:T(8,128)(2,1)S(1)} %get-tuple-element.109, s32[]{:T(128)} %get-tuple-element.108, f32[4,512,512]{1,2,0:T(8,128)} %get-tuple-element.100, f32[4,512]{1,0:T(4,128)S(1)} %get-tuple-element.101, bf16[8,4,512,16]{2,3,1,0:T(8,128)(2,1)S(1)} %get-tuple-element.118), kind=kOutput, calls=%fused_computation.13.clone.1 | convolution fusion | flops 35684352 | bytes 4334592 | tf_op jit(solution)/shard_map/while/body/eval_jaxpr/vmap(qk,ke->qe)/dot_general | solution.py:45
  93.4 4.2 %fusion.98 = (f32[4,512]{1,0:T(4,128)S(1)}, f32[4,512,512]{1,2,0:T(8,128)}) fusion(bf16[8,4,512,16]{2,3,1,0:T(8,128)(2,1)} %get-tuple-element.117, s32[]{:T(128)} %get-tuple-element.108, bf16[8,4,512,16]{2,3,1,0:T(8,128)(2,1)S(1)} %get-tuple-element.116), kind=kOutput, calls=%fused_computation.85.clone.1 | convolution fusion | flops 36700672 | bytes 4334592 | tf_op jit(solution)/shard_map/while/body/eval_jaxpr/vmap()/sub | solution.py:44
  97.6 2.6 %fusion.99 = bf16[8,4,512,16]{2,3,1,0:T(8,128)(2,1)S(1)} fusion(bf16[8,4,512,16]{2,3,1,0:T(8,128)(2,1)S(1)} %get-tuple-element.109, s32[]{:T(128)} %get-tuple-element.108, f32[4,512,512]{1,2,0:T(8,128)} %get-tuple-element.100, f32[4,512]{1,0:T(4,128)S(1)} %get-tuple-element.101, bf16[8,4,512,16]{2,3,1,0:T(8,128)(2,1)S(1)} %get-tuple-element.118), kind=kOutput, calls=%fused_computation.13.clone.1 | convolution fusion | flops 35684352 | bytes 4334592 | tf_op jit(solution)/shard_map/while/body/eval_jaxpr/vmap(qk,ke->qe)/dot_general | solution.py:45
  100.2 4.2 %fusion.98 = (f32[4,512]{1,0:T(4,128)S(1)}, f32[4,512,512]{1,2,0:T(8,128)}) fusion(bf16[8,4,512,16]{2,3,1,0:T(8,128)(2,1)} %get-tuple-element.117, s32[]{:T(128)} %get-tuple-element.108, bf16[8,4,512,16]{2,3,1,0:T(8,128)(2,1)S(1)} %get-tuple-element.116), kind=kOutput, calls=%fused_computation.85.clone.1 | convolution fusion | flops 36700672 | bytes 4334592 | tf_op jit(solution)/shard_map/while/body/eval_jaxpr/vmap()/sub | solution.py:44
  104.4 2.6 %fusion.99 = bf16[8,4,512,16]{2,3,1,0:T(8,128)(2,1)S(1)} fusion(bf16[8,4,512,16]{2,3,1,0:T(8,128)(2,1)S(1)} %get-tuple-element.109, s32[]{:T(128)} %get-tuple-element.108, f32[4,512,512]{1,2,0:T(8,128)} %get-tuple-element.100, f32[4,512]{1,0:T(4,128)S(1)} %get-tuple-element.101, bf16[8,4,512,16]{2,3,1,0:T(8,128)(2,1)S(1)} %get-tuple-element.118), kind=kOutput, calls=%fused_computation.13.clone.1 | convolution fusion | flops 35684352 | bytes 4334592 | tf_op jit(solution)/shard_map/while/body/eval_jaxpr/vmap(qk,ke->qe)/dot_general | solution.py:45
  107.0 0.5 copy.55
  107.6 0.3 reshape.138
  107.9 0.3 copy.49
  108.3 1.1 broadcast.103
  109.4 2.5 %scatter_fusion.1 = bf16[16,128,256]{2,1,0:T(8,128)(2,1)} fusion(bf16[16,128,256]{2,1,0:T(8,128)(2,1)} %broadcast.103, s32[8]{0:T(128)S(1)} %compare_select_fusion.1, bf16[8,128,256]{2,1,0:T(8,128)(2,1)S(1)} %copy.49), kind=kCustom, calls=%fused_computation.3 | custom fusion | bytes 1572896 | tf_op jit(solution)/shard_map/scatter | solution.py:20
  111.9 3.7 %all-to-all-start.1 = ((bf16[16,128,256]{2,1,0:T(8,128)(2,1)}), bf16[16,128,256]{2,1,0:T(8,128)(2,1)S(1)}, u32[]{:S(2)}, u32[]{:S(2)}) async-start(bf16[16,128,256]{2,1,0:T(8,128)(2,1)} %scatter_fusion.1), calls=%async_computation.1 | async-start | bytes 2097152 | tf_op jit(solution)/shard_map/all_to_all | solution.py:77
  115.6 0.2 copy.41
  115.9 27.4 %all-to-all-done.1 = bf16[16,128,256]{2,1,0:T(8,128)(2,1)S(1)} async-done(((bf16[16,128,256]{2,1,0:T(8,128)(2,1)}), bf16[16,128,256]{2,1,0:T(8,128)(2,1)S(1)}, u32[]{:S(2)}, u32[]{:S(2)}) %all-to-all-start.1) | async-done | bytes 1048608 | tf_op jit(solution)/shard_map/all_to_all | solution.py:77
  143.3 0.6 gather_fusion.1
  143.9 0.1 broadcast_select_fusion
  144.0 0.4 convert_reduce_fusion.1
  144.4 0.2 fusion.51
  144.6 3.5 %multiply_convert_fusion = (bf16[1024,1024]{1,0:T(8,128)(2,1)S(1)}, f32[1024,1024]{1,0:T(8,128)}) fusion(bf16[256,1024]{1,0:T(8,128)(2,1)S(1)} %copy-done, bf16[1024,256]{0,1:T(8,128)(2,1)S(1)} %get-tuple-element.64, f32[256]{0:T(256)S(1)} %copy-done.7, f32[1024]{0:T(1024)S(1)} %add_rsqrt_fusion, f32[1024]{0:T(1024)S(1)} %broadcast_multiply_fusion.1), kind=kOutput, calls=%fused_computation.39 | convolution fusion | flops 547618816 | bytes 7349248 | tf_op jit(solution)/shard_map/dot_general | solution.py:61
  148.0 0.8 convolution_convert_fusion.1
  148.8 0.5 copy-done.10
  149.4 5.6 %fusion.46 = bf16[1024,256]{1,0:T(8,128)(2,1)S(1)} fusion(f32[1024,1024]{1,0:T(8,128)} %get-tuple-element.66, bf16[1024,256]{1,0:T(8,128)(2,1)S(1)} %copy-done.5, bf16[1024,256]{1,0:T(8,128)(2,1)S(1)} %copy-done.6, bf16[1024,256]{0,1:T(8,128)(2,1)S(1)} %get-tuple-element.64, f32[256]{0:T(256)S(1)} %copy-done.7, f32[1024]{0:T(1024)S(1)} %add_rsqrt_fusion, ...), kind=kOutput, calls=%fused_computation.47 | convolution fusion | flops 1096286208 | bytes 6300672 | tf_op jit(solution)/shard_map/rf,rd->fd/dot_general | solution.py:71
  155.1 31.9 %all_to_all.25 = bf16[16,128,256]{2,1,0:T(8,128)(2,1)S(1)} all-to-all(bf16[16,128,256]{2,1,0:T(8,128)(2,1)S(1)} %pad_maximum_fusion), channel_id=1, replica_groups=mesh['group'=48,'peer'=16] {'peer'}, dimensions={0} | all-to-all | bytes 2097152 | tf_op jit(solution)/shard_map/all_to_all | solution.py:82
  187.0 0.1 convert_reduce_fusion
  187.2 27.9 %all_to_all.26 = f32[48,8,128]{2,1,0:T(8,128)S(1)} all-to-all(f32[48,8,128]{2,1,0:T(8,128)S(1)} %pad.4), channel_id=1, replica_groups=mesh['group'=48,'peer'=16] {'group'}, dimensions={0} | all-to-all | bytes 393216 | tf_op jit(solution)/shard_map/all_to_all | solution.py:82
  215.1 0.7 reshape.108
  215.8 4.8 %all-to-all-start.4 = ((f32[48,8,128]{2,1,0:T(8,128)}), f32[48,8,128]{2,1,0:T(8,128)S(1)}, u32[]{:S(2)}, u32[]{:S(2)}) async-start(f32[48,8,128]{2,1,0:T(8,128)} %reshape.108), calls=%async_computation.4 | async-start | bytes 393216 | tf_op jit(solution)/shard_map/all_to_all | solution.py:82
  220.6 2.4 fusion.47
  222.9 1.0 copy.51
  223.9 11.2 %all-to-all-done.4 = f32[48,8,128]{2,1,0:T(8,128)S(1)} async-done(((f32[48,8,128]{2,1,0:T(8,128)}), f32[48,8,128]{2,1,0:T(8,128)S(1)}, u32[]{:S(2)}, u32[]{:S(2)}) %all-to-all-start.4) | async-done | bytes 196640 | tf_op jit(solution)/shard_map/all_to_all | solution.py:82
  235.1 0.6 slice.28
  235.8 0.6 slice.30
  (37 shorter events, 0.3 us)
Async XLA Ops:
  0.6 143.9 %copy-start = (bf16[256,1024]{1,0:T(8,128)(2,1)S(1)}, bf16[256,1024]{1,0:T(8,128)(2,1)}, u32[]{:S(2)}) copy-start(bf16[256,1024]{1,0:T(8,128)(2,1)} %param.22) | copy-start | bytes 1572868
  0.6 18.5 %copy-start.8 = (s32[8]{0:T(128)S(1)}, s32[8]{0:T(128)}, u32[]{:S(2)}) copy-start(s32[8]{0:T(128)} %param.17) | copy-start | bytes 100
  1.4 47.2 %copy-start.4 = (f32[256]{0:T(256)S(1)}, f32[256]{0:T(256)}, u32[]{:S(2)}) copy-start(f32[256]{0:T(256)} %param.20) | copy-start | bytes 3076
  2.5 46.5 %copy-start.2 = (bf16[256,768]{1,0:T(8,128)(2,1)S(1)}, bf16[256,768]{1,0:T(8,128)(2,1)}, u32[]{:S(2)}) copy-start(bf16[256,768]{1,0:T(8,128)(2,1)} %param.18) | copy-start | bytes 1179652
  5.2 41.9 %all-to-all-start = ((bf16[16,128,256]{2,1,0:T(8,128)(2,1)}), bf16[16,128,256]{2,1,0:T(8,128)(2,1)S(1)}, u32[]{:S(2)}, u32[]{:S(2)}) async-start(bf16[16,128,256]{2,1,0:T(8,128)(2,1)} %scatter_fusion), calls=%async_computation | async-start | bytes 2097152 | tf_op jit(solution)/shard_map/all_to_all | solution.py:77
  107.0 8.6 %copy-start.1 = (bf16[1024,256]{1,0:T(8,128)(2,1)S(1)}, bf16[1024,256]{1,0:T(8,128)(2,1)}, u32[]{:S(2)}) copy-start(bf16[1024,256]{1,0:T(8,128)(2,1)} %param.14) | copy-start | bytes 1572868
  107.6 8.3 %copy-start.9 = (s32[8]{0:T(128)S(1)}, s32[8]{0:T(128)}, u32[]{:S(2)}) copy-start(s32[8]{0:T(128)} %param.16) | copy-start | bytes 100
  108.3 35.7 %copy-start.3 = (bf16[256,256]{1,0:T(8,128)(2,1)S(1)}, bf16[256,256]{1,0:T(8,128)(2,1)}, u32[]{:S(2)}) copy-start(bf16[256,256]{1,0:T(8,128)(2,1)} %param.19) | copy-start | bytes 393220
  109.4 35.2 %copy-start.7 = (f32[256]{0:T(256)S(1)}, f32[256]{0:T(256)}, u32[]{:S(2)}) copy-start(f32[256]{0:T(256)} %param.21) | copy-start | bytes 3076
  111.9 31.4 %all-to-all-start.1 = ((bf16[16,128,256]{2,1,0:T(8,128)(2,1)}), bf16[16,128,256]{2,1,0:T(8,128)(2,1)S(1)}, u32[]{:S(2)}, u32[]{:S(2)}) async-start(bf16[16,128,256]{2,1,0:T(8,128)(2,1)} %scatter_fusion.1), calls=%async_computation.1 | async-start | bytes 2097152 | tf_op jit(solution)/shard_map/all_to_all | solution.py:77
  144.6 3.5 %copy-start.5 = (bf16[1024,256]{1,0:T(8,128)(2,1)S(1)}, bf16[1024,256]{1,0:T(8,128)(2,1)}, u32[]{:S(2)}) copy-start(bf16[1024,256]{1,0:T(8,128)(2,1)} %param.15) | copy-start | bytes 1572868
  148.0 1.3 copy-start.10
  148.0 1.4 copy-start.6
  215.8 19.3 %all-to-all-start.4 = ((f32[48,8,128]{2,1,0:T(8,128)}), f32[48,8,128]{2,1,0:T(8,128)S(1)}, u32[]{:S(2)}, u32[]{:S(2)}) async-start(f32[48,8,128]{2,1,0:T(8,128)} %reshape.108), calls=%async_computation.4 | async-start | bytes 393216 | tf_op jit(solution)/shard_map/all_to_all | solution.py:82

commit v2 on v1

--- a/solution.py
+++ b/solution.py
@@ -1,7 +1,14 @@
+import functools
+
 import jax
 import jax.numpy as jnp
+import numpy as np
 from jax import lax
+from jax.experimental import pallas as pl
+from jax.experimental.pallas import tpu as pltpu
 from jax.sharding import PartitionSpec as P
+
+MESH = pl.DeviceIdType.MESH
 
 D = 256
 HEAD_DIM = 16
@@ -78,26 +85,123 @@
     return jnp.take(got, take_codes, axis=0).reshape(blocks.shape)
 
 
-def swap(pieces, axis):
-    return lax.all_to_all(pieces, axis, split_axis=0, concat_axis=0, tiled=True)
-
-
-def sum_grads(hid_term, out_term, peers, groups, scale):
-    units = hid_term.shape[0] // peers
-    both = jnp.concatenate(
-        [hid_term.reshape(peers, units, D), out_term.reshape(peers, units, D)], axis=1
-    ).astype(jnp.bfloat16)
-    share = jnp.sum(swap(both, "peer").astype(jnp.float32), axis=0) * scale
-    flat = share.reshape(-1, 8, 128)
-    pieces = flat.shape[0]
-    per = -(-pieces // groups)
-    padded = jnp.pad(flat, ((0, per * groups - pieces), (0, 0), (0, 0)))
-    mine = jnp.sum(
-        swap(padded, "group").reshape(groups, per, 8, 128), axis=0
-    )
-    everyone = jnp.broadcast_to(mine[None], (groups, per, 8, 128)).reshape(groups * per, 8, 128)
-    total = swap(everyone, "group")[:pieces].reshape(2 * units, D)
-    return total[:units].T, total[units:]
+def gradient_kernel(peers, xs, zs, scale, terms, out, pair_in, y_out, y_in, x_out, x_in, z_all, x_all,
+                    pair_send, pair_recv, y_send, y_recv, x_send, x_recv, z_send, z_recv, g_send, g_recv):
+    ys = peers // 2
+    peer, group = lax.axis_index("peer"), lax.axis_index("group")
+    y, core = peer // 2, peer % 2
+    x, z = group // zs, group % zs
+    rows = terms.shape[1]
+    part = rows // xs
+
+    def on_core(other):
+        return {"peer": y * 2 + other, "group": group}
+
+    def on_y(other):
+        return {"peer": other * 2 + core, "group": group}
+
+    def on_x(other):
+        return {"peer": peer, "group": other * zs + z}
+
+    def on_z(other):
+        return {"peer": peer, "group": x * zs + other}
+
+    def send(src, dst, send_sem, recv_sem, device):
+        copy = pltpu.make_async_remote_copy(
+            src_ref=src, dst_ref=dst, send_sem=send_sem, recv_sem=recv_sem,
+            device_id=device, device_id_type=MESH,
+        )
+        copy.start()
+        return copy
+
+    partners = [on_core(1 - core)]
+    partners += [on_y((y + k) % ys) for k in range(1, ys)]
+    partners += [on_x((x + k) % xs) for k in range(1, xs)]
+    partners += [on_z((z + k) % zs) for k in range(1, zs)]
+    barrier = pltpu.get_barrier_semaphore()
+    for device in partners:
+        pl.semaphore_signal(barrier, inc=1, device_id=device, device_id_type=MESH)
+    pl.semaphore_wait(barrier, len(partners))
+
+    order = list(range(1, ys)) + [0]
+    pair = {}
+    for k in order:
+        owner = (y + k) % ys
+        pair[k] = send(terms.at[owner * 2 + (1 - core)], pair_in.at[k], pair_send.at[k], pair_recv.at[k],
+                       on_core(1 - core))
+    along_y = {}
+    for k in order:
+        owner = (y + k) % ys
+        pair[k].wait_recv()
+        both = terms[owner * 2 + core].astype(jnp.float32) + pair_in[k].astype(jnp.float32)
+        if k:
+            y_out[k - 1] = both.astype(jnp.bfloat16)
+            along_y[k] = send(y_out.at[k - 1], y_in.at[k - 1], y_send.at[k - 1], y_recv.at[k - 1], on_y(owner))
+    total = both
+    for k in range(1, ys):
+        along_y[k].wait_recv()
+        total = total + y_in[k - 1].astype(jnp.float32)
+    x_out[...] = total.astype(jnp.bfloat16).reshape(xs, part, D)
+    along_x = [
+        send(x_out.at[(x + k) % xs], x_in.at[k - 1], x_send.at[k - 1], x_recv.at[k - 1], on_x((x + k) % xs))
+        for k in range(1, xs)
+    ]
+    mine = x_out[x].astype(jnp.float32)
+    for k in range(1, xs):
+        along_x[k - 1].wait_recv()
+        mine = mine + x_in[k - 1].astype(jnp.float32)
+    z_all[z] = mine.astype(jnp.bfloat16)
+    along_z = [
+        send(z_all.at[z], z_all.at[z], z_send.at[k - 1], z_recv.at[k - 1], on_z((z + k) % zs))
+        for k in range(1, zs)
+    ]
+    for copy in along_z:
+        copy.wait_recv()
+    whole = z_all[0].astype(jnp.float32)
+    for k in range(1, zs):
+        whole = whole + z_all[k].astype(jnp.float32)
+    x_all[x] = whole * scale
+    back = [
+        send(x_all.at[x], x_all.at[x], g_send.at[k - 1], g_recv.at[k - 1], on_x((x + k) % xs))
+        for k in range(1, xs)
+    ]
+    for copy in back:
+        copy.wait_recv()
+    out[...] = x_all[...].reshape(rows, D)
+    for copy in [*pair.values(), *along_y.values(), *along_x, *along_z, *back]:
+        copy.wait_send()
+
+
+def sum_grads(terms, peers, groups, scale):
+    xs = 4 if groups % 4 == 0 else 1
+    ys, zs = peers // 2, groups // xs
+    rows = terms.shape[1]
+    dma = pltpu.SemaphoreType.DMA
+    bf16 = jnp.bfloat16
+    return pl.pallas_call(
+        functools.partial(gradient_kernel, peers, xs, zs, scale),
+        out_shape=jax.ShapeDtypeStruct((rows, D), jnp.float32),
+        in_specs=[pl.BlockSpec(memory_space=pltpu.VMEM)],
+        out_specs=pl.BlockSpec(memory_space=pltpu.VMEM),
+        scratch_shapes=[
+            pltpu.VMEM((ys, rows, D), bf16),
+            pltpu.VMEM((ys - 1, rows, D), bf16),
+            pltpu.VMEM((ys - 1, rows, D), bf16),
+            pltpu.VMEM((xs, rows // xs, D), bf16),
+            pltpu.VMEM((max(xs - 1, 1), rows // xs, D), bf16),
+            pltpu.VMEM((zs, rows // xs, D), bf16),
+            pltpu.VMEM((xs, rows // xs, D), jnp.float32),
+            dma((ys,)), dma((ys,)),
+            dma((ys - 1,)), dma((ys - 1,)),
+            dma((max(xs - 1, 1),)), dma((max(xs - 1, 1),)),
+            dma((max(zs - 1, 1),)), dma((max(zs - 1, 1),)),
+            dma((max(xs - 1, 1),)), dma((max(xs - 1, 1),)),
+        ],
+        compiler_params=pltpu.CompilerParams(
+            collective_id=0, has_side_effects=True, vmem_limit_bytes=32 << 20
+        ),
+        cost_estimate=pl.CostEstimate(flops=1 << 24, bytes_accessed=64 << 20, transcendentals=0),
+    )(terms)
 
 
 def per_device(
@@ -110,7 +214,7 @@
     block_rows = rows // blocks_here
     slots = peers * ((blocks_here + peers - 1) // peers)
     patch = PATCH_BLOCKS * block_rows
-    grad_scale = 1.0 / jnp.sqrt(jnp.float32(rows * peers * groups))
+    grad_scale = float(1.0 / np.sqrt(np.float32(rows * peers * groups)))
     feats = redeal(points, dest_code, src_code, slots, block_rows)
     att = attend(feats, w_qkv, norm_attn, rows, patch)
     att = redeal(att, src_code, dest_code, slots, block_rows)
@@ -118,7 +222,12 @@
         points.astype(jnp.float32) + jnp.dot(att, w_out, preferred_element_type=jnp.float32)
     ).astype(jnp.bfloat16)
     result, hid_term, out_term = mlp_terms(hidden_state, cotangent, norm_mlp, w_hidden, w_output)
-    hidden_grad, output_grad = sum_grads(hid_term, out_term, peers, groups, grad_scale)
+    units = hid_term.shape[0] // peers
+    terms = jnp.concatenate(
+        [hid_term.reshape(peers, units, D), out_term.reshape(peers, units, D)], axis=1
+    ).astype(jnp.bfloat16)
+    sums = sum_grads(terms, peers, groups, grad_scale)
+    hidden_grad, output_grad = sums[:units].T, sums[units:]
     return (result, hidden_grad, output_grad)
 
 

time: 238 us -> 199 us (0.84)
  the two profiles are of different devices: /device:TPU:1 before, /device:TPU:16 now
where the time goes in v2:
time: 199 us; the launch traced here: 198 us
  matrix products  66.2 us (33%)
  waiting for transfers between devices  49.4 us (25%)
  Pallas kernels  44.6 us (22%)
  starting transfers between devices  19.4 us (10%)
  local copies, waits for them, and re-layouts  14.8 us (7%)
  other arithmetic  2.36 us (1%)
    all_to_all x2, waiting for transfers between devices, redeal(): got = lax.all_to_all(buf, 'peer', split_axis=0, concat_axis=0, tiled=True)  49.4 us
    pallas_call x1, Pallas kernels, sum_grads(): pl.pallas_call(functools.partial(gradient_kernel, peers, xs, zs, scale),...  44.6 us
    sub x8, matrix products, one_head(): probs = jax.nn.softmax(scores, axis=-1).astype(jnp.bfloat16)  33.9 us
    dot_general x8, matrix products, one_head(): jnp.einsum('qk,ke->qe', probs, triple[2], preferred_element_type=jnp.floa...  20.7 us
    all_to_all x2, starting transfers between devices, redeal(): got = lax.all_to_all(buf, 'peer', split_axis=0, concat_axis=0, tiled=True)  19.4 us
    dot_general x1, matrix products, mlp_terms(): jnp.einsum('rf,rd->fd', dpre, second, preferred_element_type=jnp.float32)  5.72 us
    scatter x2, local copies, waits for them, and re-layouts, pack_blocks(): jnp.zeros((slots, block_rows, width), arr.dtype).at[codes].set(pieces)  5.18 us
  transfers between devices with their start and end apart: 2, of which 2 were waited for; matrix products, arithmetic and copies ran while one was open for 0% of the time, Pallas kernels for 0%

profile of v2, /device:TPU:16, one launch (start us, length us, event | category | flops | bytes accessed | tf_op | source)
XLA Modules:
  0.0 197.7 jit_solution(7472843315193932437)
XLA Ops:
  0.6 0.0 copy-start
  0.7 0.7 compare_select_fusion
  1.4 1.1 broadcast.95.clone
  2.5 2.7 %scatter_fusion = bf16[16,128,256]{2,1,0:T(8,128)(2,1)} fusion(bf16[16,128,256]{2,1,0:T(8,128)(2,1)} %broadcast.95.clone, s32[8]{0:T(128)S(1)} %compare_select_fusion, bf16[8,128,256]{2,1,0:T(8,128)(2,1)} %bitcast.86), kind=kCustom, calls=%fused_computation.2 | custom fusion | bytes 1572896 | tf_op jit(solution)/shard_map/scatter | solution.py:27
  5.2 12.8 %all-to-all-start = ((bf16[16,128,256]{2,1,0:T(8,128)(2,1)}), bf16[16,128,256]{2,1,0:T(8,128)(2,1)S(1)}, u32[]{:S(2)}, u32[]{:S(2)}) async-start(bf16[16,128,256]{2,1,0:T(8,128)(2,1)} %scatter_fusion), calls=%async_computation | async-start | bytes 2097152 | tf_op jit(solution)/shard_map/all_to_all | solution.py:84
  18.1 24.9 %all-to-all-done = bf16[16,128,256]{2,1,0:T(8,128)(2,1)S(1)} async-done(((bf16[16,128,256]{2,1,0:T(8,128)(2,1)}), bf16[16,128,256]{2,1,0:T(8,128)(2,1)S(1)}, u32[]{:S(2)}, u32[]{:S(2)}) %all-to-all-start) | async-done | bytes 1048608 | tf_op jit(solution)/shard_map/all_to_all | solution.py:84
  43.0 0.6 gather_fusion
  43.6 0.3 fusion.67
  43.9 0.1 select_convert_fusion
  44.0 0.5 multiply_reduce_fusion.1
  44.5 0.3 fusion.56
  44.9 0.6 convolution_convert_fusion
  45.5 0.1 fusion.77
  45.6 0.2 copy.32
  45.8 0.4 reshape.87
  46.2 0.9 copy.33
  47.0 0.2 copy.34
  47.3 0.4 reshape.88
  47.6 0.1 copy.35
  47.7 0.2 copy.30
  47.9 0.4 reshape.86
  48.3 0.1 copy.31
  48.4 54.6 %while.10 = (s32[]{:T(128)}, bf16[8,4,512,16]{2,3,1,0:T(8,128)(2,1)S(1)}, bf16[8,4,512,16]{2,3,1,0:T(8,128)(2,1)S(1)}, bf16[8,4,512,16]{2,3,1,0:T(8,128)(2,1)}, bf16[8,4,512,16]{2,3,1,0:T(8,128)(2,1)S(1)}, /*index=5*/s32[]{:T(128)}) while((s32[]{:T(128)}, bf16[8,4,512,16]{2,3,1,0:T(8,128)(2,1)S(1)}, bf16[8,4,512,16]{2,3,1,0:T(8,128)(2,1)S(1)}, ...), condition=%wide.region_6.8_spmd, body=%wide.region_3.7_spmd.sunk | while | flops 72385024 | bytes 8669253 | solution.py:56
  48.4 4.2 %fusion.98 = (f32[4,512]{1,0:T(4,128)S(1)}, f32[4,512,512]{1,2,0:T(8,128)}) fusion(bf16[8,4,512,16]{2,3,1,0:T(8,128)(2,1)} %get-tuple-element.114, s32[]{:T(128)} %get-tuple-element.105, bf16[8,4,512,16]{2,3,1,0:T(8,128)(2,1)S(1)} %get-tuple-element.113), kind=kOutput, calls=%fused_computation.84.clone.1 | convolution fusion | flops 36700672 | bytes 4334592 | tf_op jit(solution)/shard_map/while/body/eval_jaxpr/vmap()/sub | solution.py:51
  52.6 2.6 %fusion.99 = bf16[8,4,512,16]{2,3,1,0:T(8,128)(2,1)S(1)} fusion(bf16[8,4,512,16]{2,3,1,0:T(8,128)(2,1)S(1)} %get-tuple-element.106, s32[]{:T(128)} %get-tuple-element.105, f32[4,512,512]{1,2,0:T(8,128)} %get-tuple-element.97, f32[4,512]{1,0:T(4,128)S(1)} %get-tuple-element.98, bf16[8,4,512,16]{2,3,1,0:T(8,128)(2,1)S(1)} %get-tuple-element.115), kind=kOutput, calls=%fused_computation.13.clone.1 | convolution fusion | flops 35684352 | bytes 4334592 | tf_op jit(solution)/shard_map/while/body/eval_jaxpr/vmap(qk,ke->qe)/dot_general | solution.py:52
  55.2 4.2 %fusion.98 = (f32[4,512]{1,0:T(4,128)S(1)}, f32[4,512,512]{1,2,0:T(8,128)}) fusion(bf16[8,4,512,16]{2,3,1,0:T(8,128)(2,1)} %get-tuple-element.114, s32[]{:T(128)} %get-tuple-element.105, bf16[8,4,512,16]{2,3,1,0:T(8,128)(2,1)S(1)} %get-tuple-element.113), kind=kOutput, calls=%fused_computation.84.clone.1 | convolution fusion | flops 36700672 | bytes 4334592 | tf_op jit(solution)/shard_map/while/body/eval_jaxpr/vmap()/sub | solution.py:51
  59.5 2.6 %fusion.99 = bf16[8,4,512,16]{2,3,1,0:T(8,128)(2,1)S(1)} fusion(bf16[8,4,512,16]{2,3,1,0:T(8,128)(2,1)S(1)} %get-tuple-element.106, s32[]{:T(128)} %get-tuple-element.105, f32[4,512,512]{1,2,0:T(8,128)} %get-tuple-element.97, f32[4,512]{1,0:T(4,128)S(1)} %get-tuple-element.98, bf16[8,4,512,16]{2,3,1,0:T(8,128)(2,1)S(1)} %get-tuple-element.115), kind=kOutput, calls=%fused_computation.13.clone.1 | convolution fusion | flops 35684352 | bytes 4334592 | tf_op jit(solution)/shard_map/while/body/eval_jaxpr/vmap(qk,ke->qe)/dot_general | solution.py:52
  62.0 4.2 %fusion.98 = (f32[4,512]{1,0:T(4,128)S(1)}, f32[4,512,512]{1,2,0:T(8,128)}) fusion(bf16[8,4,512,16]{2,3,1,0:T(8,128)(2,1)} %get-tuple-element.114, s32[]{:T(128)} %get-tuple-element.105, bf16[8,4,512,16]{2,3,1,0:T(8,128)(2,1)S(1)} %get-tuple-element.113), kind=kOutput, calls=%fused_computation.84.clone.1 | convolution fusion | flops 36700672 | bytes 4334592 | tf_op jit(solution)/shard_map/while/body/eval_jaxpr/vmap()/sub | solution.py:51
  66.3 2.6 %fusion.99 = bf16[8,4,512,16]{2,3,1,0:T(8,128)(2,1)S(1)} fusion(bf16[8,4,512,16]{2,3,1,0:T(8,128)(2,1)S(1)} %get-tuple-element.106, s32[]{:T(128)} %get-tuple-element.105, f32[4,512,512]{1,2,0:T(8,128)} %get-tuple-element.97, f32[4,512]{1,0:T(4,128)S(1)} %get-tuple-element.98, bf16[8,4,512,16]{2,3,1,0:T(8,128)(2,1)S(1)} %get-tuple-element.115), kind=kOutput, calls=%fused_computation.13.clone.1 | convolution fusion | flops 35684352 | bytes 4334592 | tf_op jit(solution)/shard_map/while/body/eval_jaxpr/vmap(qk,ke->qe)/dot_general | solution.py:52
  68.9 4.2 %fusion.98 = (f32[4,512]{1,0:T(4,128)S(1)}, f32[4,512,512]{1,2,0:T(8,128)}) fusion(bf16[8,4,512,16]{2,3,1,0:T(8,128)(2,1)} %get-tuple-element.114, s32[]{:T(128)} %get-tuple-element.105, bf16[8,4,512,16]{2,3,1,0:T(8,128)(2,1)S(1)} %get-tuple-element.113), kind=kOutput, calls=%fused_computation.84.clone.1 | convolution fusion | flops 36700672 | bytes 4334592 | tf_op jit(solution)/shard_map/while/body/eval_jaxpr/vmap()/sub | solution.py:51
  73.1 2.6 %fusion.99 = bf16[8,4,512,16]{2,3,1,0:T(8,128)(2,1)S(1)} fusion(bf16[8,4,512,16]{2,3,1,0:T(8,128)(2,1)S(1)} %get-tuple-element.106, s32[]{:T(128)} %get-tuple-element.105, f32[4,512,512]{1,2,0:T(8,128)} %get-tuple-element.97, f32[4,512]{1,0:T(4,128)S(1)} %get-tuple-element.98, bf16[8,4,512,16]{2,3,1,0:T(8,128)(2,1)S(1)} %get-tuple-element.115), kind=kOutput, calls=%fused_computation.13.clone.1 | convolution fusion | flops 35684352 | bytes 4334592 | tf_op jit(solution)/shard_map/while/body/eval_jaxpr/vmap(qk,ke->qe)/dot_general | solution.py:52
  75.7 4.2 %fusion.98 = (f32[4,512]{1,0:T(4,128)S(1)}, f32[4,512,512]{1,2,0:T(8,128)}) fusion(bf16[8,4,512,16]{2,3,1,0:T(8,128)(2,1)} %get-tuple-element.114, s32[]{:T(128)} %get-tuple-element.105, bf16[8,4,512,16]{2,3,1,0:T(8,128)(2,1)S(1)} %get-tuple-element.113), kind=kOutput, calls=%fused_computation.84.clone.1 | convolution fusion | flops 36700672 | bytes 4334592 | tf_op jit(solution)/shard_map/while/body/eval_jaxpr/vmap()/sub | solution.py:51
  79.9 2.6 %fusion.99 = bf16[8,4,512,16]{2,3,1,0:T(8,128)(2,1)S(1)} fusion(bf16[8,4,512,16]{2,3,1,0:T(8,128)(2,1)S(1)} %get-tuple-element.106, s32[]{:T(128)} %get-tuple-element.105, f32[4,512,512]{1,2,0:T(8,128)} %get-tuple-element.97, f32[4,512]{1,0:T(4,128)S(1)} %get-tuple-element.98, bf16[8,4,512,16]{2,3,1,0:T(8,128)(2,1)S(1)} %get-tuple-element.115), kind=kOutput, calls=%fused_computation.13.clone.1 | convolution fusion | flops 35684352 | bytes 4334592 | tf_op jit(solution)/shard_map/while/body/eval_jaxpr/vmap(qk,ke->qe)/dot_general | solution.py:52
  82.5 4.2 %fusion.98 = (f32[4,512]{1,0:T(4,128)S(1)}, f32[4,512,512]{1,2,0:T(8,128)}) fusion(bf16[8,4,512,16]{2,3,1,0:T(8,128)(2,1)} %get-tuple-element.114, s32[]{:T(128)} %get-tuple-element.105, bf16[8,4,512,16]{2,3,1,0:T(8,128)(2,1)S(1)} %get-tuple-element.113), kind=kOutput, calls=%fused_computation.84.clone.1 | convolution fusion | flops 36700672 | bytes 4334592 | tf_op jit(solution)/shard_map/while/body/eval_jaxpr/vmap()/sub | solution.py:51
  86.7 2.6 %fusion.99 = bf16[8,4,512,16]{2,3,1,0:T(8,128)(2,1)S(1)} fusion(bf16[8,4,512,16]{2,3,1,0:T(8,128)(2,1)S(1)} %get-tuple-element.106, s32[]{:T(128)} %get-tuple-element.105, f32[4,512,512]{1,2,0:T(8,128)} %get-tuple-element.97, f32[4,512]{1,0:T(4,128)S(1)} %get-tuple-element.98, bf16[8,4,512,16]{2,3,1,0:T(8,128)(2,1)S(1)} %get-tuple-element.115), kind=kOutput, calls=%fused_computation.13.clone.1 | convolution fusion | flops 35684352 | bytes 4334592 | tf_op jit(solution)/shard_map/while/body/eval_jaxpr/vmap(qk,ke->qe)/dot_general | solution.py:52
  89.3 4.2 %fusion.98 = (f32[4,512]{1,0:T(4,128)S(1)}, f32[4,512,512]{1,2,0:T(8,128)}) fusion(bf16[8,4,512,16]{2,3,1,0:T(8,128)(2,1)} %get-tuple-element.114, s32[]{:T(128)} %get-tuple-element.105, bf16[8,4,512,16]{2,3,1,0:T(8,128)(2,1)S(1)} %get-tuple-element.113), kind=kOutput, calls=%fused_computation.84.clone.1 | convolution fusion | flops 36700672 | bytes 4334592 | tf_op jit(solution)/shard_map/while/body/eval_jaxpr/vmap()/sub | solution.py:51
  93.6 2.6 %fusion.99 = bf16[8,4,512,16]{2,3,1,0:T(8,128)(2,1)S(1)} fusion(bf16[8,4,512,16]{2,3,1,0:T(8,128)(2,1)S(1)} %get-tuple-element.106, s32[]{:T(128)} %get-tuple-element.105, f32[4,512,512]{1,2,0:T(8,128)} %get-tuple-element.97, f32[4,512]{1,0:T(4,128)S(1)} %get-tuple-element.98, bf16[8,4,512,16]{2,3,1,0:T(8,128)(2,1)S(1)} %get-tuple-element.115), kind=kOutput, calls=%fused_computation.13.clone.1 | convolution fusion | flops 35684352 | bytes 4334592 | tf_op jit(solution)/shard_map/while/body/eval_jaxpr/vmap(qk,ke->qe)/dot_general | solution.py:52
  96.1 4.2 %fusion.98 = (f32[4,512]{1,0:T(4,128)S(1)}, f32[4,512,512]{1,2,0:T(8,128)}) fusion(bf16[8,4,512,16]{2,3,1,0:T(8,128)(2,1)} %get-tuple-element.114, s32[]{:T(128)} %get-tuple-element.105, bf16[8,4,512,16]{2,3,1,0:T(8,128)(2,1)S(1)} %get-tuple-element.113), kind=kOutput, calls=%fused_computation.84.clone.1 | convolution fusion | flops 36700672 | bytes 4334592 | tf_op jit(solution)/shard_map/while/body/eval_jaxpr/vmap()/sub | solution.py:51
  100.4 2.6 %fusion.99 = bf16[8,4,512,16]{2,3,1,0:T(8,128)(2,1)S(1)} fusion(bf16[8,4,512,16]{2,3,1,0:T(8,128)(2,1)S(1)} %get-tuple-element.106, s32[]{:T(128)} %get-tuple-element.105, f32[4,512,512]{1,2,0:T(8,128)} %get-tuple-element.97, f32[4,512]{1,0:T(4,128)S(1)} %get-tuple-element.98, bf16[8,4,512,16]{2,3,1,0:T(8,128)(2,1)S(1)} %get-tuple-element.115), kind=kOutput, calls=%fused_computation.13.clone.1 | convolution fusion | flops 35684352 | bytes 4334592 | tf_op jit(solution)/shard_map/while/body/eval_jaxpr/vmap(qk,ke->qe)/dot_general | solution.py:52
  103.0 0.5 copy.43
  103.5 0.0 copy-start.9
  103.5 0.3 reshape.121
  103.9 0.3 copy.37
  104.2 0.0 copy-start.3
  104.2 1.1 broadcast.95
  105.3 2.4 %scatter_fusion.1 = bf16[16,128,256]{2,1,0:T(8,128)(2,1)} fusion(bf16[16,128,256]{2,1,0:T(8,128)(2,1)} %broadcast.95, s32[8]{0:T(128)S(1)} %compare_select_fusion.1, bf16[8,128,256]{2,1,0:T(8,128)(2,1)S(1)} %copy.37), kind=kCustom, calls=%fused_computation.3 | custom fusion | bytes 1572896 | tf_op jit(solution)/shard_map/scatter | solution.py:27
  107.8 6.6 %all-to-all-start.1 = ((bf16[16,128,256]{2,1,0:T(8,128)(2,1)}), bf16[16,128,256]{2,1,0:T(8,128)(2,1)S(1)}, u32[]{:S(2)}, u32[]{:S(2)}) async-start(bf16[16,128,256]{2,1,0:T(8,128)(2,1)} %scatter_fusion.1), calls=%async_computation.1 | async-start | bytes 2097152 | tf_op jit(solution)/shard_map/all_to_all | solution.py:84
  114.3 0.2 copy.29
  114.6 24.5 %all-to-all-done.1 = bf16[16,128,256]{2,1,0:T(8,128)(2,1)S(1)} async-done(((bf16[16,128,256]{2,1,0:T(8,128)(2,1)}), bf16[16,128,256]{2,1,0:T(8,128)(2,1)S(1)}, u32[]{:S(2)}, u32[]{:S(2)}) %all-to-all-start.1) | async-done | bytes 1048608 | tf_op jit(solution)/shard_map/all_to_all | solution.py:84
  139.1 0.6 gather_fusion.1
  139.7 0.1 broadcast_select_fusion
  139.8 0.4 convert_reduce_fusion
  140.2 0.2 fusion.51
  140.3 0.0 copy-done
  140.4 0.0 copy-start.6
  140.4 3.5 %multiply_convert_fusion = (bf16[1024,1024]{1,0:T(8,128)(2,1)S(1)}, f32[1024,1024]{1,0:T(8,128)}) fusion(bf16[256,1024]{1,0:T(8,128)(2,1)S(1)} %copy-done, bf16[1024,256]{0,1:T(8,128)(2,1)S(1)} %get-tuple-element.61, f32[256]{0:T(256)S(1)} %copy-done.7, f32[1024]{0:T(1024)S(1)} %add_rsqrt_fusion, f32[1024]{0:T(1024)S(1)} %broadcast_multiply_fusion), kind=kOutput, calls=%fused_computation.39 | convolution fusion | flops 547618816 | bytes 7349248 | tf_op jit(solution)/shard_map/dot_general | solution.py:68
  143.8 0.8 convolution_convert_fusion.1
  144.6 0.3 copy-done.5
  144.9 0.8 fusion.47
  145.6 5.7 %fusion.46 = bf16[1024,256]{1,0:T(8,128)(2,1)S(1)} fusion(f32[1024,1024]{1,0:T(8,128)} %get-tuple-element.63, bf16[1024,256]{1,0:T(8,128)(2,1)} %param.15, bf16[1024,256]{1,0:T(8,128)(2,1)S(1)} %copy-done.5, bf16[1024,256]{0,1:T(8,128)(2,1)S(1)} %get-tuple-element.61, f32[256]{0:T(256)S(1)} %copy-done.7, f32[1024]{0:T(1024)S(1)} %add_rsqrt_fusion, ...), kind=kOutput, calls=%fused_computation.46 | convolution fusion | flops 1096286208 | bytes 6300672 | tf_op jit(solution)/shard_map/rf,rd->fd/dot_general | solution.py:78
  151.4 0.1 pad_maximum_fusion.terms
  151.5 44.6 %shard_map.121 = f32[128,256]{1,0:T(8,128)S(1)} custom-call(bf16[16,128,256]{2,1,0:T(8,128)(2,1)S(1)} %pad_maximum_fusion.terms), custom_call_target="tpu_custom_call" | custom-call | flops 16777216 | bytes 67108864 | tf_op jit(solution)/shard_map/pallas_call | solution.py:181
  196.1 0.7 fusion.78
  196.7 1.0 copy.39
  (24 shorter events, 0.1 us)
Async XLA Ops:
  0.6 139.7 %copy-start = (bf16[256,1024]{1,0:T(8,128)(2,1)S(1)}, bf16[256,1024]{1,0:T(8,128)(2,1)}, u32[]{:S(2)}) copy-start(bf16[256,1024]{1,0:T(8,128)(2,1)} %param.22) | copy-start | bytes 1572868
  0.6 17.4 %copy-start.8 = (s32[8]{0:T(128)S(1)}, s32[8]{0:T(128)}, u32[]{:S(2)}) copy-start(s32[8]{0:T(128)} %param.17) | copy-start | bytes 100
  1.4 43.1 %copy-start.4 = (f32[256]{0:T(256)S(1)}, f32[256]{0:T(256)}, u32[]{:S(2)}) copy-start(f32[256]{0:T(256)} %param.20) | copy-start | bytes 3076
  2.5 42.4 %copy-start.2 = (bf16[256,768]{1,0:T(8,128)(2,1)S(1)}, bf16[256,768]{1,0:T(8,128)(2,1)}, u32[]{:S(2)}) copy-start(bf16[256,768]{1,0:T(8,128)(2,1)} %param.18) | copy-start | bytes 1179652
  5.2 37.8 %all-to-all-start = ((bf16[16,128,256]{2,1,0:T(8,128)(2,1)}), bf16[16,128,256]{2,1,0:T(8,128)(2,1)S(1)}, u32[]{:S(2)}, u32[]{:S(2)}) async-start(bf16[16,128,256]{2,1,0:T(8,128)(2,1)} %scatter_fusion), calls=%async_computation | async-start | bytes 2097152 | tf_op jit(solution)/shard_map/all_to_all | solution.py:84
  103.0 11.4 %copy-start.1 = (bf16[1024,256]{1,0:T(8,128)(2,1)S(1)}, bf16[1024,256]{1,0:T(8,128)(2,1)}, u32[]{:S(2)}) copy-start(bf16[1024,256]{1,0:T(8,128)(2,1)} %param.14) | copy-start | bytes 1572868
  103.5 11.0 %copy-start.9 = (s32[8]{0:T(128)S(1)}, s32[8]{0:T(128)}, u32[]{:S(2)}) copy-start(s32[8]{0:T(128)} %param.16) | copy-start | bytes 100
  104.2 35.6 %copy-start.3 = (bf16[256,256]{1,0:T(8,128)(2,1)S(1)}, bf16[256,256]{1,0:T(8,128)(2,1)}, u32[]{:S(2)}) copy-start(bf16[256,256]{1,0:T(8,128)(2,1)} %param.19) | copy-start | bytes 393220
  105.3 35.0 %copy-start.7 = (f32[256]{0:T(256)S(1)}, f32[256]{0:T(256)}, u32[]{:S(2)}) copy-start(f32[256]{0:T(256)} %param.21) | copy-start | bytes 3076
  107.8 31.3 %all-to-all-start.1 = ((bf16[16,128,256]{2,1,0:T(8,128)(2,1)}), bf16[16,128,256]{2,1,0:T(8,128)(2,1)S(1)}, u32[]{:S(2)}, u32[]{:S(2)}) async-start(bf16[16,128,256]{2,1,0:T(8,128)(2,1)} %scatter_fusion.1), calls=%async_computation.1 | async-start | bytes 2097152 | tf_op jit(solution)/shard_map/all_to_all | solution.py:84
  140.4 3.5 %copy-start.6 = (bf16[1024,256]{1,0:T(8,128)(2,1)S(1)}, bf16[1024,256]{1,0:T(8,128)(2,1)}, u32[]{:S(2)}) copy-start(bf16[1024,256]{1,0:T(8,128)(2,1)} %param.15) | copy-start | bytes 1572868
  143.8 1.0 copy-start.5

commit v3 on v2

--- a/solution.py
+++ b/solution.py
@@ -13,6 +13,7 @@
 D = 256
 HEAD_DIM = 16
 PATCH_BLOCKS = 4
+LANES = 128
 
 
 def layer_norm(v):
@@ -21,46 +22,131 @@
     return centre * lax.rsqrt(spread + 1e-05)
 
 
-def pack_blocks(arr, codes, slots, block_rows):
-    width = arr.shape[1]
-    pieces = arr.reshape(codes.shape[0], block_rows, width)
-    return jnp.zeros((slots, block_rows, width), arr.dtype).at[codes].set(pieces)
-
-
-def split_heads(mat, patches, patch, heads):
-    return (
-        mat.reshape(patches, patch, heads, HEAD_DIM)
-        .transpose(0, 2, 1, 3)
-        .reshape(patches * heads, patch, HEAD_DIM)
+def start_send(src, dst, send_sem, recv_sem, device):
+    copy = pltpu.make_async_remote_copy(
+        src_ref=src, dst_ref=dst, send_sem=send_sem, recv_sem=recv_sem,
+        device_id=device, device_id_type=MESH,
     )
-
-
-def patch_attention(qkv, rows, patch):
-    heads = D // HEAD_DIM
-    patches = rows // patch
-    query = split_heads(qkv[:, :D], patches, patch, heads)
-    keys = split_heads(qkv[:, D : 2 * D], patches, patch, heads)
-    values = split_heads(qkv[:, 2 * D :], patches, patch, heads)
-    factor = 1.0 / jnp.sqrt(jnp.float32(HEAD_DIM))
-
-    def one_head(triple):
-        scores = (
-            jnp.einsum("qe,ke->qk", triple[0], triple[1], preferred_element_type=jnp.float32)
-            * factor
-        )
-        probs = jax.nn.softmax(scores, axis=-1).astype(jnp.bfloat16)
-        return jnp.einsum("qk,ke->qe", probs, triple[2], preferred_element_type=jnp.float32).astype(
-            jnp.bfloat16
-        )
-
-    mixed = lax.map(one_head, (query, keys, values), batch_size=4)
-    return mixed.reshape(patches, heads, patch, HEAD_DIM).transpose(0, 2, 1, 3).reshape(rows, D)
-
-
-def attend(feats, w_qkv, norm_attn, rows, patch):
-    normed = (layer_norm(feats.astype(jnp.float32)) * norm_attn).astype(jnp.bfloat16)
-    qkv = jnp.dot(normed, w_qkv, preferred_element_type=jnp.float32).astype(jnp.bfloat16)
-    return patch_attention(qkv, rows, patch)
+    copy.start()
+    return copy
+
+
+def block_for(codes, peer):
+    which = jnp.int32(0)
+    for i in range(codes.shape[0]):
+        which = jnp.where(codes[i] == peer, i, which)
+    return which
+
+
+def heads_of_lanes(qkv, att, first_row, rows, lanes):
+    head_of_lane = lax.broadcasted_iota(jnp.int32, (1, LANES), 1) // HEAD_DIM
+    ones = jnp.ones((rows, LANES), jnp.bfloat16)
+    factor = 1.4426950408889634 / HEAD_DIM**0.5
+    tile = rows // 2
+    zero = jnp.bfloat16(0)
+
+    def one_head(head, carry):
+        mine = head_of_lane == head
+        keys = qkv[first_row : first_row + rows, D + lanes : D + lanes + LANES]
+        values = qkv[first_row : first_row + rows, 2 * D + lanes : 2 * D + lanes + LANES]
+        values = jnp.concatenate([jnp.where(mine, values, zero), ones], axis=1)
+        for start in range(first_row, first_row + rows, tile):
+            query = jnp.where(mine, qkv[start : start + tile, lanes : lanes + LANES], zero)
+            scores = lax.dot_general(
+                query, keys, (((1,), (1,)), ((), ())), preferred_element_type=jnp.float32
+            )
+            top = jnp.max(scores, axis=1, keepdims=True)
+            weights = jnp.exp2((scores - top) * factor).astype(jnp.bfloat16)
+            mixed = jnp.dot(weights, values, preferred_element_type=jnp.float32)
+            att[start : start + tile] += mixed[:, :LANES] / mixed[:, LANES:]
+        return carry
+
+    lax.fori_loop(0, LANES // HEAD_DIM, one_head, 0, unroll=LANES // HEAD_DIM)
+
+
+def attention_kernel(peers, points, dest, src, w_qkv, w_out, norm_attn, out, normed, stage, got, feats,
+                     qkv, att, mixed, back_stage, back, whole, send_sem, recv_sem, back_send, back_recv):
+    group, me = lax.axis_index("group"), lax.axis_index("peer")
+    blocks, block_rows = points.shape[0], points.shape[1]
+    patch = PATCH_BLOCKS * block_rows
+    others = [(me + k) % peers for k in range(1, peers)]
+
+    def at(peer):
+        return {"group": group, "peer": peer}
+
+    barrier = pltpu.get_barrier_semaphore()
+    for peer in others:
+        pl.semaphore_signal(barrier, inc=1, device_id=at(peer), device_id_type=MESH)
+    for i in range(blocks):
+        normed[i] = (layer_norm(points[i].astype(jnp.float32)) * norm_attn[...]).astype(jnp.bfloat16)
+    for k, peer in enumerate(others):
+        stage[k] = normed[block_for(dest, peer)]
+    got[me] = normed[block_for(dest, me)]
+    pl.semaphore_wait(barrier, peers - 1)
+    sent = [
+        start_send(stage.at[k], got.at[me], send_sem.at[k], recv_sem.at[k], at(peer))
+        for k, peer in enumerate(others)
+    ]
+    for copy in sent:
+        copy.wait_recv()
+    for j in range(blocks):
+        feats[j * block_rows : (j + 1) * block_rows] = got[src[j]]
+    qkv[...] = jnp.dot(feats[...], w_qkv[...], preferred_element_type=jnp.float32).astype(jnp.bfloat16)
+    for part in range(D // LANES):
+        att[...] = jnp.zeros_like(att)
+        for first_row in range(0, blocks * block_rows, patch):
+            heads_of_lanes(qkv, att, first_row, patch, part * LANES)
+        mixed[part] = att[...].astype(jnp.bfloat16).reshape(blocks, block_rows, LANES)
+        for k, peer in enumerate(others):
+            back_stage[part, k] = mixed[part, block_for(src, peer)]
+            sent.append(
+                start_send(back_stage.at[part, k], back.at[part, me], back_send.at[part, k],
+                           back_recv.at[part, k], at(peer))
+            )
+        back[part, me] = mixed[part, block_for(src, me)]
+    for copy in sent[peers - 1 :]:
+        copy.wait_recv()
+    for part in range(D // LANES):
+        for i in range(blocks):
+            whole[i * block_rows : (i + 1) * block_rows, part * LANES : (part + 1) * LANES] = back[part, dest[i]]
+    added = jnp.dot(whole[...], w_out[...], preferred_element_type=jnp.float32)
+    for i in range(blocks):
+        out[i] = (points[i].astype(jnp.float32) + added[i * block_rows : (i + 1) * block_rows]).astype(jnp.bfloat16)
+    for copy in sent:
+        copy.wait_send()
+
+
+def attend(points, dest_code, src_code, w_qkv, w_out, norm_attn, peers):
+    blocks = dest_code.shape[0]
+    rows = points.shape[0]
+    block_rows = rows // blocks
+    parts = D // LANES
+    vmem, smem = pl.BlockSpec(memory_space=pltpu.VMEM), pl.BlockSpec(memory_space=pltpu.SMEM)
+    dma, bf16 = pltpu.SemaphoreType.DMA, jnp.bfloat16
+    return pl.pallas_call(
+        functools.partial(attention_kernel, peers),
+        out_shape=jax.ShapeDtypeStruct((blocks, block_rows, D), bf16),
+        in_specs=[vmem, smem, smem, vmem, vmem, vmem],
+        out_specs=vmem,
+        scratch_shapes=[
+            pltpu.VMEM((blocks, block_rows, D), bf16),
+            pltpu.VMEM((peers - 1, block_rows, D), bf16),
+            pltpu.VMEM((peers, block_rows, D), bf16),
+            pltpu.VMEM((rows, D), bf16),
+            pltpu.VMEM((rows, 3 * D), bf16),
+            pltpu.VMEM((rows, LANES), jnp.float32),
+            pltpu.VMEM((parts, blocks, block_rows, LANES), bf16),
+            pltpu.VMEM((parts, peers - 1, block_rows, LANES), bf16),
+            pltpu.VMEM((parts, peers, block_rows, LANES), bf16),
+            pltpu.VMEM((rows, D), bf16),
+            dma((peers - 1,)), dma((peers - 1,)),
+            dma((parts, peers - 1)), dma((parts, peers - 1)),
+        ],
+        compiler_params=pltpu.CompilerParams(
+            collective_id=1, has_side_effects=True, vmem_limit_bytes=48 << 20
+        ),
+        cost_estimate=pl.CostEstimate(flops=1 << 32, bytes_accessed=4 << 20, transcendentals=1 << 23),
+    )(points.reshape(blocks, block_rows, D), dest_code, src_code, w_qkv, w_out, norm_attn.reshape(1, D)).reshape(rows, D)
 
 
 def mlp_terms(hidden_state, cot, norm_mlp, w_hidden, w_output):
@@ -77,12 +163,6 @@
     dpre = gelu_back(dact)[0].astype(jnp.bfloat16)
     hid_term = jnp.einsum("rf,rd->fd", dpre, second, preferred_element_type=jnp.float32)
     return (result, hid_term, out_term)
-
-
-def redeal(blocks, send_codes, take_codes, slots, block_rows):
-    buf = pack_blocks(blocks, send_codes, slots, block_rows)
-    got = lax.all_to_all(buf, "peer", split_axis=0, concat_axis=0, tiled=True)
-    return jnp.take(got, take_codes, axis=0).reshape(blocks.shape)
 
 
 def gradient_kernel(peers, xs, zs, scale, terms, out, pair_in, y_out, y_in, x_out, x_in, z_all, x_all,
@@ -209,18 +289,9 @@
 ):
     peers = lax.axis_size("peer")
     groups = lax.axis_size("group")
-    blocks_here = dest_code.shape[0]
     rows = points.shape[0]
-    block_rows = rows // blocks_here
-    slots = peers * ((blocks_here + peers - 1) // peers)
-    patch = PATCH_BLOCKS * block_rows
     grad_scale = float(1.0 / np.sqrt(np.float32(rows * peers * groups)))
-    feats = redeal(points, dest_code, src_code, slots, block_rows)
-    att = attend(feats, w_qkv, norm_attn, rows, patch)
-    att = redeal(att, src_code, dest_code, slots, block_rows)
-    hidden_state = (
-        points.astype(jnp.float32) + jnp.dot(att, w_out, preferred_element_type=jnp.float32)
-    ).astype(jnp.bfloat16)
+    hidden_state = attend(points, dest_code, src_code, w_qkv, w_out, norm_attn, peers)
     result, hid_term, out_term = mlp_terms(hidden_state, cotangent, norm_mlp, w_hidden, w_output)
     units = hid_term.shape[0] // peers
     terms = jnp.concatenate(

time: 199 us -> 138 us (0.69)
  Pallas kernels: 44.6 us -> 113 us
  matrix products: 66.2 us -> 11.1 us
  waiting for transfers between devices: 49.4 us -> 0 us
  starting transfers between devices: 19.4 us -> 0 us
  local copies, waits for them, and re-layouts: 14.8 us -> 11.3 us
    pallas_call x0 -> x1, Pallas kernels: none -> 69.5 us  [attend(): pl.pallas_call(functools.partial(attention_kernel, peers), out_shape=jax....]
    all_to_all x2 -> x0, waiting for transfers between devices: 49.4 us -> none  [redeal(): got = lax.all_to_all(buf, 'peer', split_axis=0, concat_axis=0, tiled=True)]
    sub x8 -> x0, matrix products: 33.9 us -> none  [one_head(): probs = jax.nn.softmax(scores, axis=-1).astype(jnp.bfloat16)]
    all_to_all x2 -> x0, starting transfers between devices: 19.4 us -> none  [redeal(): got = lax.all_to_all(buf, 'peer', split_axis=0, concat_axis=0, tiled=True)]
    dot_general x10 -> x1, matrix products: 21.6 us -> 3.18 us  [mlp_terms(): jnp.einsum('rd,fd->rf', cot, w_output, preferred_element_type=jnp.float32)]
    dot_general x0 -> x1, local copies, waits for them, and re-layouts: none -> 5.39 us  [mlp_terms(): pre = jnp.dot(second, w_hidden, preferred_element_type=jnp.float32)]
    scatter x2 -> x0, local copies, waits for them, and re-layouts: 5.18 us -> none  [pack_blocks(): jnp.zeros((slots, block_rows, width), arr.dtype).at[codes].set(pieces)]
    dot_general x1, matrix products: 5.72 us -> 0.71 us  [mlp_terms(): jnp.einsum('rf,rd->fd', dpre, second, preferred_element_type=jnp.float32)]
  transfers between devices with their start and end apart: 2 -> 0, of which waited for: 2 -> 0; matrix products, arithmetic and copies ran while one was open for 0% -> 0% of each run, Pallas kernels for 0% -> 0%
where the time goes in v3:
time: 138 us
  Pallas kernels  113 us (82%)
  local copies, waits for them, and re-layouts  11.3 us (8%)
  matrix products  11.1 us (8%)
    pallas_call x1, Pallas kernels, attend(): pl.pallas_call(functools.partial(attention_kernel, peers), out_shape=jax....  69.5 us
    pallas_call x1, Pallas kernels, sum_grads(): pl.pallas_call(functools.partial(gradient_kernel, peers, xs, zs, scale),...  43.8 us
    dot_general x1, local copies, waits for them, and re-layouts, mlp_terms(): pre = jnp.dot(second, w_hidden, preferred_element_type=jnp.float32)  5.39 us
    unnamed x24, local copies, waits for them, and re-layouts  5.27 us
    dot_general x1, matrix products, mlp_terms(): jnp.einsum('rf,rd->fd', act, cot, preferred_element_type=jnp.float32)  4.13 us
    dot_general x1, matrix products, mlp_terms(): jnp.einsum('rd,fd->rf', cot, w_output, preferred_element_type=jnp.float32)  3.18 us

profile of v3, /device:TPU:16, one launch (start us, length us, event | category | flops | bytes accessed | tf_op | source)
XLA Modules:
  0.0 137.8 jit_solution(3668624922653259276)
XLA Ops:
  0.6 0.0 copy-start
  0.6 0.0 copy-start.1
  0.7 1.1 copy-done.1
  1.7 0.0 copy-start.2
  1.8 1.0 copy-done.2
  2.7 0.0 copy-start.3
  2.7 0.9 copy-done.3
  3.6 0.0 copy-start.4
  3.7 0.7 copy-done.4
  4.3 0.0 copy-start.5
  4.3 0.7 copy-done.5
  5.0 0.0 copy-start.6
  5.0 0.7 copy-done.6
  5.6 0.0 copy-start.10
  5.6 0.0 copy-start.9
  5.6 69.5 %shard_map.121 = bf16[8,128,256]{2,1,0:T(8,128)(2,1)S(1)} custom-call(bf16[8,128,256]{2,1,0:T(8,128)(2,1)S(1)} %bitcast.43, s32[8]{0:T(128)S(1)} %copy-done.5, s32[8]{0:T(128)S(1)} %copy-done.6, bf16[256,768]{1,0:T(8,128)(2,1)S(1)} %copy-done.2, bf16[256,256]{1,0:T(8,128)(2,1)S(1)} %copy-done.3, f32[1,256]{1,0:T(1,128)S(1)} %bitcast.44), custom_call_target="tpu_custom_call" | custom-call | flops 4294967296 | bytes 4194304 | tf_op jit(solution)/shard_map/pallas_call | solution.py:126
  75.1 0.2 convert_reduce_fusion
  75.3 0.4 multiply_reduce_fusion
  75.7 0.0 copy-done.10
  75.7 0.3 fusion.20
  76.1 0.0 copy-done.9
  76.1 0.0 copy-start.11
  76.1 0.8 fusion.26
  76.9 0.0 copy-done
  76.9 0.3 copy-done.11
  77.2 0.0 copy-start.7
  77.2 3.2 %fusion.6 = bf16[1024,1024]{1,0:T(8,128)(2,1)S(1)} fusion(f32[1024,1024]{0,1:T(8,128)S(1)} %fusion.26, bf16[1024,256]{1,0:T(8,128)(2,1)S(1)} %copy-done.11, bf16[1024,256]{1,0:T(8,128)(2,1)S(1)} %copy-done), kind=kOutput, calls=%fused_computation.9 | convolution fusion | flops 557842432 | bytes 7340032 | tf_op jit(solution)/shard_map/rd,fd->rf/dot_general | solution.py:162
  80.3 0.0 copy-done.7
  80.3 0.3 multiply_convert_fusion
  80.7 0.7 convolution_convert_fusion.1
  81.4 5.4 %copy.17 = f32[1024,1024]{1,0:T(8,128)} copy(f32[1024,1024]{0,1:T(8,128)} %copy-done.7) | data formatting | bytes 8388608 | tf_op jit(solution)/shard_map/dot_general | solution.py:154
  86.8 0.0 copy-start.8
  86.8 4.1 %convolution_convert_fusion = bf16[1024,256]{1,0:T(8,128)(2,1)S(1)} fusion(bf16[1024,256]{1,0:T(8,128)(2,1)S(1)} %copy-done, f32[1024,1024]{1,0:T(8,128)} %copy.17), kind=kOutput, calls=%fused_computation.22 | convolution fusion | flops 546570240 | bytes 5242880 | tf_op jit(solution)/shard_map/rf,rd->fd/dot_general | solution.py:161
  90.9 0.1 pad_maximum_fusion.terms
  91.0 43.8 %shard_map.122 = f32[128,256]{1,0:T(8,128)S(1)} custom-call(bf16[16,128,256]{2,1,0:T(8,128)(2,1)S(1)} %pad_maximum_fusion.terms), custom_call_target="tpu_custom_call" | custom-call | flops 16777216 | bytes 67108864 | tf_op jit(solution)/shard_map/pallas_call | solution.py:261
  134.9 0.7 fusion.25
  135.5 0.0 copy-done.8
  135.5 2.3 %fusion.17 = bf16[1024,256]{1,0:T(8,128)(2,1)} fusion(bf16[1024,256]{1,0:T(8,128)(2,1)S(1)} %copy-done.11, f32[1024,1024]{1,0:T(8,128)S(1)} %copy-done.8, bf16[1024,256]{1,0:T(8,128)(2,1)S(1)} %bitcast.42), kind=kOutput, calls=%fused_computation.24 | convolution fusion | flops 547094528 | bytes 5767168 | tf_op jit(solution)/shard_map/dot_general | solution.py:159
  (2 shorter events, 0.0 us)
Async XLA Ops:
  0.6 76.2 %copy-start = (bf16[1024,256]{1,0:T(8,128)(2,1)S(1)}, bf16[1024,256]{1,0:T(8,128)(2,1)}, u32[]{:S(2)}) copy-start(bf16[1024,256]{1,0:T(8,128)(2,1)} %param.11) | copy-start | bytes 1572868
  0.6 1.1 copy-start.1
  1.7 1.0 copy-start.2
  2.7 0.9 copy-start.3
  3.6 0.7 copy-start.4
  4.3 0.7 copy-start.5
  5.0 0.7 copy-start.6
  5.6 70.1 %copy-start.10 = (f32[256]{0:T(256)S(1)}, f32[256]{0:T(256)}, u32[]{:S(2)}) copy-start(f32[256]{0:T(256)} %param.17) | copy-start | bytes 3076
  5.6 70.5 %copy-start.9 = (bf16[256,1024]{1,0:T(8,128)(2,1)S(1)}, bf16[256,1024]{1,0:T(8,128)(2,1)}, u32[]{:S(2)}) copy-start(bf16[256,1024]{1,0:T(8,128)(2,1)} %param.18) | copy-start | bytes 1572868
  76.1 1.0 copy-start.11
  77.2 3.2 %copy-start.7 = (f32[1024,1024]{0,1:T(8,128)}, f32[1024,1024]{0,1:T(8,128)S(1)}, u32[]{:S(2)}) copy-start(f32[1024,1024]{0,1:T(8,128)S(1)} %fusion.26) | copy-start | bytes 12582916
  86.8 48.7 %copy-start.8 = (f32[1024,1024]{1,0:T(8,128)S(1)}, f32[1024,1024]{1,0:T(8,128)}, u32[]{:S(2)}) copy-start(f32[1024,1024]{1,0:T(8,128)} %copy.17) | copy-start | bytes 12582916

commit v4 on v0

v4 whole, which is shorter than its diff:
```python
import functools

import jax
import jax.numpy as jnp
import numpy as np
from jax import lax
from jax.experimental import pallas as pl
from jax.experimental.pallas import tpu as pltpu
from jax.sharding import PartitionSpec as P

D = 256
HEAD_DIM = 16
PATCH_BLOCKS = 4
LANES = 128
HALF = 64
UNITS = 256
MESH = pl.DeviceIdType.MESH
F32, BF16 = jnp.float32, jnp.bfloat16


def layer_norm(v):
    centre = v - jnp.mean(v, axis=-1, keepdims=True)
    spread = jnp.mean(centre * centre, axis=-1, keepdims=True)
    return centre * lax.rsqrt(spread + 1e-05)


def dot(a, b):
    return jnp.dot(a, b, preferred_element_type=F32)


def dot_rows(a, b):
    return lax.dot_general(a, b, (((1,), (1,)), ((), ())), preferred_element_type=F32)


def gelu_and_slope(x):
    root = 0.7978845608028654
    square = x * x
    bend = jnp.tanh(x * (root + (root * 0.044715) * square))
    half = 0.5 + 0.5 * bend
    slope = half + (0.5 * x) * (1.0 - bend * bend) * (root + (3 * root * 0.044715) * square)
    return x * half, slope


def start_send(src, dst, send_sem, recv_sem, device):
    copy = pltpu.make_async_remote_copy(
        src_ref=src, dst_ref=dst, send_sem=send_sem, recv_sem=recv_sem,
        device_id=device, device_id_type=MESH,
    )
    copy.start()
    return copy


def block_for(codes, peer):
    which = jnp.int32(0)
    for i in range(codes.shape[0]):
        which = jnp.where(codes[i] == peer, i, which)
    return which


def some_heads(qkv, att, first_row, rows, lanes, heads):
    head_of_lane = lax.broadcasted_iota(jnp.int32, (1, LANES), 1) // HEAD_DIM
    ones = jnp.ones((rows, LANES), BF16)
    factor = 1.4426950408889634 / HEAD_DIM**0.5
    tile = rows // 2
    zero = jnp.bfloat16(0)

    def one_head(head, carry):
        mine = head_of_lane == head
        keys = qkv[first_row : first_row + rows, D + lanes : D + lanes + LANES]
        values = qkv[first_row : first_row + rows, 2 * D + lanes : 2 * D + lanes + LANES]
        values = jnp.concatenate([jnp.where(mine, values, zero), ones], axis=1)
        for start in range(first_row, first_row + rows, tile):
            query = jnp.where(mine, qkv[start : start + tile, lanes : lanes + LANES], zero)
            scores = dot_rows(query, keys)
            top = jnp.max(scores, axis=1, keepdims=True)
            weights = jnp.exp2((scores - top) * factor).astype(BF16)
            mixed = dot(weights, values)
            att[start : start + tile] += mixed[:, :LANES] / mixed[:, LANES:]
        return carry

    lax.fori_loop(heads[0], heads[1], one_head, 0, unroll=heads[1] - heads[0])


def swap_halves(upper, lower, first):
    low = lax.broadcasted_iota(jnp.int32, (1, LANES), 1) < HALF
    if first:
        return jnp.where(low, upper, pltpu.roll(lower, HALF, 1))
    return jnp.where(low, pltpu.roll(upper, HALF, 1), lower)


def block_kernel(peers, xs, zs, scale, points_any, cot_any, dest, src, w_qkv_any, w_out_any, norm_attn,
                 norm_mlp, w_hidden_any, w_output_any, out_any, hidden_grad, output_grad,
                 points, cot, w_qkv, w_out, w_hidden, w_output, w_hidden_t, w_output_t,
                 normed, stage, got, feats, qkv, att, packed, back_stage, back, whole, hidden, second,
                 dact, result, answer, terms, pair_in, x_out, x_in, y_out, y_in, z_all, x_all,
                 load_sem, send_sem, recv_sem, back_send, back_recv, pair_send, pair_recv,
                 x_send, x_recv, y_send, y_recv, z_send, z_recv, g_send, g_recv, out_sem):
    loads = [
        pltpu.make_async_copy(a, b, load_sem.at[i])
        for i, (a, b) in enumerate(
            [(points_any, points), (w_qkv_any, w_qkv), (w_out_any, w_out), (cot_any, cot),
             (w_hidden_any, w_hidden), (w_output_any, w_output)]
        )
    ]
    for load in loads:
        load.start()
    group, me = lax.axis_index("group"), lax.axis_index("peer")
    ys = peers // 2
    y, core = me // 2, me % 2
    x, z = group // zs, group % zs
    blocks, block_rows = points.shape[0], points.shape[1]
    rows = blocks * block_rows
    patch = PATCH_BLOCKS * block_rows
    others = [(me + k) % peers for k in range(1, peers)]

    def at(peer):
        return {"group": group, "peer": peer}

    def on_x(other):
        return {"group": other * zs + z, "peer": me}

    def on_z(other):
        return {"group": x * zs + other, "peer": me}

    partners = [at(peer) for peer in others]
    partners += [on_x((x + k) % xs) for k in range(1, xs)]
    partners += [on_z((z + k) % zs) for k in range(1, zs)]
    barrier = pltpu.get_barrier_semaphore()
    for device in partners:
        pl.semaphore_signal(barrier, inc=1, device_id=device, device_id_type=MESH)

    loads[0].wait()
    for i in range(blocks):
        normed[i] = (layer_norm(points[i].astype(F32)) * norm_attn[...]).astype(BF16)
    for k, peer in enumerate(others):
        stage[k] = normed[block_for(dest, peer)]
    got[me] = normed[block_for(dest, me)]
    pl.semaphore_wait(barrier, len(partners))
    sent = [
        start_send(stage.at[k], got.at[me], send_sem.at[k], recv_sem.at[k], at(peer))
        for k, peer in enumerate(others)
    ]
    for load in loads[1:]:
        load.wait()
    w_hidden_t[...] = w_hidden[...].astype(F32).T.astype(BF16)
    w_output_t[...] = w_output[...].astype(F32).T.astype(BF16)
    dact[...] = dot_rows(w_output[...], cot[...])
    for copy in sent:
        copy.wait_recv()

    for j in range(blocks):
        feats[j * block_rows : (j + 1) * block_rows] = got[src[j]]
    qkv[...] = dot(feats[...], w_qkv[...]).astype(BF16)
    returned = []
    per_part = LANES // HEAD_DIM // 2
    for part in range(D // HALF):
        group_lanes, first = part // 2 * LANES, part % 2 == 0
        head = part % 2 * per_part
        att[...] = jnp.zeros_like(att)
        for first_row in range(0, rows, patch):
            some_heads(qkv, att, first_row, patch, group_lanes, (head, head + per_part))
        for j in range(blocks):
            start = j * block_rows
            packed[part, j] = swap_halves(
                att[start : start + HALF], att[start + HALF : start + block_rows], first
            ).astype(BF16)
        for k, peer in enumerate(others):
            back_stage[part, k] = packed[part, block_for(src, peer)]
            returned.append(
                start_send(back_stage.at[part, k], back.at[part, me], back_send.at[part, k],
                           back_recv.at[part, k], at(peer))
            )
        back[part, me] = packed[part, block_for(src, me)]
    for copy in returned:
        copy.wait_recv()
    for i in range(blocks):
        start = i * block_rows
        for lanes in range(D // LANES):
            even = back[2 * lanes, dest[i]].astype(F32)
            odd = back[2 * lanes + 1, dest[i]].astype(F32)
            cols = slice(lanes * LANES, (lanes + 1) * LANES)
            whole[start : start + HALF, cols] = swap_halves(even, odd, True).astype(BF16)
            whole[start + HALF : start + block_rows, cols] = swap_halves(even, odd, False).astype(BF16)
    for i in range(blocks):
        span = slice(i * block_rows, (i + 1) * block_rows)
        h = (points[i].astype(F32) + dot(whole[span], w_out[...])).astype(BF16)
        hidden[span] = h
        second[span] = (layer_norm(h.astype(F32)) * norm_mlp[...]).astype(BF16)

    chunks = w_hidden_t.shape[0] // UNITS
    share = UNITS * peers // w_hidden_t.shape[0]
    units = UNITS // share
    pairs = share // 2
    quarter = 2 * units // xs
    pair, along_x = [], []

    def to_pair(chunk):
        for j in range(pairs):
            pair.append(
                start_send(terms.at[chunk * share + 2 * j + (1 - core)], pair_in.at[chunk * pairs + j],
                           pair_send.at[chunk * pairs + j], pair_recv.at[chunk * pairs + j], at(y * 2 + 1 - core))
            )

    def to_x(chunk):
        for j in range(pairs):
            pair[chunk * pairs + j].wait_recv()
            both = terms[chunk * share + 2 * j + core].astype(F32) + pair_in[chunk * pairs + j].astype(F32)
            both = both.astype(BF16)
            for t in range(xs):
                x_out[chunk, t, j] = both[t * quarter : (t + 1) * quarter]
        for k in range(1, xs):
            along_x.append(
                start_send(x_out.at[chunk, (x + k) % xs], x_in.at[chunk, k - 1], x_send.at[chunk, k - 1],
                           x_recv.at[chunk, k - 1], on_x((x + k) % xs))
            )

    tile = UNITS
    for chunk in range(chunks):
        span = slice(chunk * UNITS, (chunk + 1) * UNITS)
        out_sum = hid_sum = None
        for start in range(0, rows, tile):
            these = slice(start, start + tile)
            act, slope = gelu_and_slope(dot_rows(w_hidden_t[span], second[these]))
            act = act.astype(BF16)
            dpre = (dact[span, these] * slope).astype(BF16)
            added = dot(w_output_t[:, span], act)
            result[:, these] = added if chunk == 0 else result[:, these] + added
            out_part, hid_part = dot(act, cot[these]), dot(dpre, second[these])
            out_sum = out_part if out_sum is None else out_sum + out_part
            hid_sum = hid_part if hid_sum is None else hid_sum + hid_part
        for j in range(share):
            mine = slice(j * units, (j + 1) * units)
            terms[chunk * share + j, :units] = hid_sum[mine].astype(BF16)
            terms[chunk * share + j, units:] = out_sum[mine].astype(BF16)
        to_pair(chunk)
        if chunk:
            to_x(chunk - 1)
    to_x(chunks - 1)
    for start in range(0, rows, tile):
        these = slice(start, start + tile)
        answer[these] = (hidden[these].astype(F32) + result[:, these].T).astype(BF16)
    store = pltpu.make_async_copy(answer, out_any, out_sem)
    store.start()

    for copy in along_x:
        copy.wait_recv()
    for chunk in range(chunks):
        for j in range(pairs):
            mine = x_out[chunk, x, j].astype(F32)
            for k in range(xs - 1):
                mine = mine + x_in[chunk, k, j].astype(F32)
            y_out[chunk * pairs + j] = mine.astype(BF16)
    along_y = [
        start_send(y_out.at[(y + k) % ys], y_in.at[k - 1], y_send.at[k - 1], y_recv.at[k - 1],
                   at((y + k) % ys * 2 + core))
        for k in range(1, ys)
    ]
    mine = y_out[y].astype(F32)
    for k, copy in enumerate(along_y):
        copy.wait_recv()
        mine = mine + y_in[k].astype(F32)
    z_all[z] = mine.astype(BF16)
    along_z = [
        start_send(z_all.at[z], z_all.at[z], z_send.at[k - 1], z_recv.at[k - 1], on_z((z + k) % zs))
        for k in range(1, zs)
    ]
    for copy in along_z:
        copy.wait_recv()
    total = z_all[0].astype(F32)
    for k in range(1, zs):
        total = total + z_all[k].astype(F32)
    x_all[x] = total * scale
    last = [
        start_send(x_all.at[x], x_all.at[x], g_send.at[k - 1], g_recv.at[k - 1], on_x((x + k) % xs))
        for k in range(1, xs)
    ]
    for copy in last:
        copy.wait_recv()
    sums = x_all[...].reshape(2 * units, D)
    hidden_grad[...] = sums[:units].T
    output_grad[...] = sums[units:]
    for copy in [*sent, *returned, *pair, *along_x, *along_y, *along_z, *last]:
        copy.wait_send()
    store.wait()


def per_device(
    points, cotangent, dest_code, src_code, w_qkv, w_out, norm_attn, norm_mlp, w_hidden, w_output
):
    peers, groups = lax.axis_size("peer"), lax.axis_size("group")
    xs = 4 if groups % 4 == 0 else 1
    ys, zs = peers // 2, groups // xs
    blocks, rows = dest_code.shape[0], points.shape[0]
    block_rows, ff = rows // blocks, w_output.shape[0]
    scale = float(1.0 / np.sqrt(np.float32(rows * peers * groups)))
    units = ff // peers
    chunks, pairs = ff // UNITS, UNITS // units // 2
    quarter = 2 * units // xs
    parts = D // HALF
    vmem, smem = pl.BlockSpec(memory_space=pltpu.VMEM), pl.BlockSpec(memory_space=pltpu.SMEM)
    far = pl.BlockSpec(memory_space=pl.ANY)
    dma = pltpu.SemaphoreType.DMA
    some = max(xs - 1, 1)
    held = lambda shape, dtype=BF16: pltpu.VMEM(shape, dtype)
    result, hidden_grad, output_grad = pl.pallas_call(
        functools.partial(block_kernel, peers, xs, zs, scale),
        out_shape=(
            jax.ShapeDtypeStruct((rows, D), BF16),
            jax.ShapeDtypeStruct((D, units), F32),
            jax.ShapeDtypeStruct((units, D), F32),
        ),
        in_specs=[far, far, smem, smem, far, far, vmem, vmem, far, far],
        out_specs=(far, vmem, vmem),
        scratch_shapes=[
            held((blocks, block_rows, D)), held((rows, D)), held((D, 3 * D)), held((D, D)),
            held((D, ff)), held((ff, D)), held((ff, D)), held((D, ff)),
            held((blocks, block_rows, D)), held((peers - 1, block_rows, D)), held((peers, block_rows, D)),
            held((rows, D)), held((rows, 3 * D)), held((rows, LANES), F32),
            held((parts, blocks, block_rows // 2, LANES)),
            held((parts, peers - 1, block_rows // 2, LANES)),
            held((parts, peers, block_rows // 2, LANES)),
            held((rows, D)), held((rows, D)), held((rows, D)),
            held((ff, rows), F32), held((D, rows), F32), held((rows, D)),
            held((peers, 2 * units, D)), held((ys, 2 * units, D)),
            held((chunks, xs, pairs, quarter, D)), held((chunks, some, pairs, quarter, D)),
            held((ys, quarter, D)), held((ys - 1, quarter, D)),
            held((zs, quarter, D)), held((xs, quarter, D), F32),
            dma((6,)), dma((peers - 1,)), dma((peers - 1,)),
            dma((parts, peers - 1)), dma((parts, peers - 1)),
            dma((ys,)), dma((ys,)), dma((chunks, some)), dma((chunks, some)),
            dma((ys - 1,)), dma((ys - 1,)), dma((max(zs - 1, 1),)), dma((max(zs - 1, 1),)),
            dma((some,)), dma((some,)), dma(()),
        ],
        compiler_params=pltpu.CompilerParams(
            collective_id=0, has_side_effects=True, vmem_limit_bytes=56 << 20
        ),
        cost_estimate=pl.CostEstimate(flops=1 << 33, bytes_accessed=4 << 20, transcendentals=1 << 23),
    )(points.reshape(blocks, block_rows, D), cotangent, dest_code, src_code, w_qkv, w_out,
      norm_attn.reshape(1, D), norm_mlp.reshape(1, D), w_hidden, w_output)
    return result, hidden_grad, output_grad


def solution(mesh):
    return jax.shard_map(
        per_device,
        mesh=mesh,
        in_specs=(
            P(("group", "peer"), None),
            P(("group", "peer"), None),
            P(("group", "peer")),
            P(("group", "peer")),
            P(),
            P(),
            P(),
            P(),
            P(),
            P(),
        ),
        out_specs=(P(("group", "peer"), None), P(None, "peer"), P("peer", None)),
        check_vma=False,
    )
```

time: 501 us -> 113 us (0.23); the launches traced: 494 us -> 113 us
  waiting for transfers between devices: 350 us -> 0 us
  Pallas kernels: 0 us -> 108 us
  matrix products: 74.7 us -> 0 us
  starting transfers between devices: 25 us -> 0 us
  local copies, waits for them, and re-layouts: 26 us -> 4.15 us
  between operations: 14 us -> 0.64 us
    psum x1 -> x0, waiting for transfers between devices: 209 us -> none  [per_device(): hid_full, out_full = lax.psum((hid_term, out_term), 'group')]
    pallas_call x0 -> x1, Pallas kernels: none -> 108 us  [per_device(): pl.pallas_call(functools.partial(block_kernel, peers, xs, zs, scale), out...]
    reduce_scatter x2 -> x0, waiting for transfers between devices: 86.7 us -> none  [the longest x1 68.5 us: per_device(): lax.psum_scatter(hid_full, 'peer', scatter_dimension=1, tiled=True)]
    all_to_all x3 -> x0, waiting for transfers between devices: 54 us -> none  [the longest x1 29.6 us: per_device(): lax.all_to_all(out_buf, 'peer', split_axis=0, concat_axis=0, tiled=True)]
    dot_general x14 -> x0, matrix products: 40.8 us -> none  [the longest x8 26 us: one_head(): jnp.einsum('qk,ke->qe', probs, triple[2], preferred_element_type=jnp.floa...]
    sub x8 -> x0, matrix products: 33.8 us -> none  [one_head(): probs = jax.nn.softmax(scores, axis=-1).astype(jnp.bfloat16)]
    all_to_all x3 -> x0, starting transfers between devices: 24.7 us -> none  [the longest x1 14 us: per_device(): lax.all_to_all(point_buf, 'peer', split_axis=0, concat_axis=0, tiled=True)]
    scatter x3 -> x0, local copies, waits for them, and re-layouts: 7.67 us -> none  [pack_blocks(): jnp.zeros((slots, block_rows, width), arr.dtype).at[codes].set(pieces)]
  transfers between devices with their start and end apart: 6 -> 0, of which waited for: 5 -> 0; matrix products, arithmetic and copies ran while one was open for 18% -> 0% of each run, Pallas kernels for 0% -> 0%
where the time goes in v4:
time: 113 us
  Pallas kernels  108 us (96%)
  local copies, waits for them, and re-layouts  4.15 us (4%)
    pallas_call x1, Pallas kernels, per_device(): pl.pallas_call(functools.partial(block_kernel, peers, xs, zs, scale), out...  108 us
    unnamed x4, local copies, waits for them, and re-layouts  2.53 us

profile of v4, /device:TPU:1, one launch (start us, length us, event | category | flops | bytes accessed | tf_op | source)
XLA Modules:
  0.0 112.6 jit_solution(10301845729355826021)
XLA Ops:
  0.6 107.8 %shard_map.121 = (bf16[1024,256]{1,0:T(8,128)(2,1)}, f32[256,64]{1,0:T(8,128)}, f32[64,256]{1,0:T(8,128)}) custom-call(bf16[8,128,256]{2,1,0:T(8,128)(2,1)} %bitcast.3, bf16[1024,256]{1,0:T(8,128)(2,1)} %cot_any.1, s32[8]{0:T(128)} %dest.1, s32[8]{0:T(128)} %src.1, bf16[256,768]{1,0:T(8,128)(2,1)} %w_qkv_any.1, bf16[256,256]{1,0:T(8,128)(2,1)} %w_out_any.1, ...), custom_call_target="tpu_custom_call" | custom-call | flops 8589934592 | bytes 4194304 | tf_op jit(solution)/shard_map/pallas_call | solution.py:305
  108.4 1.6 %copy.13 = f32[256,64]{0,1:T(8,128)} copy(f32[256,64]{1,0:T(8,128)} %get-tuple-element.4) | data formatting | bytes 131072 | tf_op jit(solution)/shard_map/pallas_call | solution.py:305
  110.1 0.0 copy-start
  110.1 1.9 %copy.16 = bf16[1024,256]{1,0:T(8,128)(2,1)} copy(bf16[1024,256]{1,0:T(8,128)(2,1)} %get-tuple-element.9) | data formatting | bytes 1048576
  112.0 0.0 copy-done
  112.0 0.6 copy.17
Async XLA Ops:
  110.1 1.9 %copy-start = (f32[64,256]{1,0:T(8,128)S(1)}, f32[64,256]{1,0:T(8,128)}, u32[]{:S(2)}) copy-start(f32[64,256]{1,0:T(8,128)} %get-tuple-element.11) | copy-start | bytes 196612

commit v5 on v4

v5 whole, which is shorter than its diff:
```python
import functools

import jax
import jax.numpy as jnp
import numpy as np
from jax import lax
from jax.experimental import pallas as pl
from jax.experimental.pallas import tpu as pltpu
from jax.sharding import PartitionSpec as P

D = 256
HEAD_DIM = 16
PATCH_BLOCKS = 4
LANES = 128
PARTS = 4
SENDS = 2
UNITS = 256
MESH = pl.DeviceIdType.MESH
F32, BF16 = jnp.float32, jnp.bfloat16


def layer_norm(v):
    centre = v - jnp.mean(v, axis=-1, keepdims=True)
    spread = jnp.mean(centre * centre, axis=-1, keepdims=True)
    return centre * lax.rsqrt(spread + 1e-05)


def dot(a, b):
    return jnp.dot(a, b, preferred_element_type=F32)


def dot_rows(a, b):
    return lax.dot_general(a, b, (((1,), (1,)), ((), ())), preferred_element_type=F32)


def gelu_and_slope(x):
    root = 0.7978845608028654
    square = x * x
    bend = jnp.tanh(x * (root + (root * 0.044715) * square))
    half = 0.5 + 0.5 * bend
    slope = half + (0.5 * x) * (1.0 - bend * bend) * (root + (3 * root * 0.044715) * square)
    return x * half, slope


def start_send(src, dst, send_sem, recv_sem, device):
    copy = pltpu.make_async_remote_copy(
        src_ref=src, dst_ref=dst, send_sem=send_sem, recv_sem=recv_sem,
        device_id=device, device_id_type=MESH,
    )
    copy.start()
    return copy


def block_for(codes, peer):
    which = jnp.int32(0)
    for i in range(codes.shape[0]):
        which = jnp.where(codes[i] == peer, i, which)
    return which


def some_queries(qkv, att, first_key, keys_count, first_query, queries, first_out):
    head_of_lane = lax.broadcasted_iota(jnp.int32, (1, LANES), 1) // HEAD_DIM
    ones = jnp.ones((keys_count, LANES), BF16)
    factor = 1.4426950408889634 / HEAD_DIM**0.5
    zero = jnp.bfloat16(0)
    patch = slice(first_key, first_key + keys_count)
    these = slice(first_query, first_query + queries)
    outs = slice(first_out, first_out + queries)
    for lanes in range(0, D, LANES):

        def one_head(head, carry):
            mine = head_of_lane == head
            keys = qkv[patch, D + lanes : D + lanes + LANES]
            values = qkv[patch, 2 * D + lanes : 2 * D + lanes + LANES]
            values = jnp.concatenate([jnp.where(mine, values, zero), ones], axis=1)
            query = jnp.where(mine, qkv[these, lanes : lanes + LANES], zero)
            scores = dot_rows(query, keys)
            top = jnp.max(scores, axis=1, keepdims=True)
            weights = jnp.exp2((scores - top) * factor).astype(BF16)
            mixed = dot(weights, values)
            att[outs, lanes : lanes + LANES] += mixed[:, :LANES] / mixed[:, LANES:]
            return carry

        lax.fori_loop(0, LANES // HEAD_DIM, one_head, 0, unroll=LANES // HEAD_DIM)


def block_kernel(peers, xs, zs, scale, points_any, cot_any, dest, src, w_qkv_any, w_out_any, norm_attn,
                 norm_mlp, w_hidden_any, w_output_any, out_any, hidden_grad, output_grad,
                 points, cot, w_qkv, w_out, w_hidden, w_output, w_hidden_t, w_output_t,
                 cot_parts, normed, stage, got, feats, qkv, att, packed, back_stage, back, second,
                 dact, result, answer, out_acc, hid_acc, terms, pair_in, x_out, x_in, y_out, y_in, z_all, x_all,
                 load_sem, send_sem, recv_sem, back_send, back_recv, pair_send, pair_recv,
                 x_send, x_recv, y_send, y_recv, z_send, z_recv, g_send, g_recv, out_sem):
    loads = [
        pltpu.make_async_copy(a, b, load_sem.at[i])
        for i, (a, b) in enumerate(
            [(points_any, points), (w_qkv_any, w_qkv), (w_out_any, w_out), (cot_any, cot),
             (w_hidden_any, w_hidden), (w_output_any, w_output)]
        )
    ]
    for load in loads:
        load.start()
    group, me = lax.axis_index("group"), lax.axis_index("peer")
    ys = peers // 2
    y, core = me // 2, me % 2
    x, z = group // zs, group % zs
    blocks, block_rows = points.shape[0], points.shape[1]
    rows = blocks * block_rows
    patch = PATCH_BLOCKS * block_rows
    others = [(me + k) % peers for k in range(1, peers)]

    def at(peer):
        return {"group": group, "peer": peer}

    def on_x(other):
        return {"group": other * zs + z, "peer": me}

    def on_z(other):
        return {"group": x * zs + other, "peer": me}

    partners = [at(peer) for peer in others]
    partners += [on_x((x + k) % xs) for k in range(1, xs)]
    partners += [on_z((z + k) % zs) for k in range(1, zs)]
    barrier = pltpu.get_barrier_semaphore()
    for device in partners:
        pl.semaphore_signal(barrier, inc=1, device_id=device, device_id_type=MESH)

    loads[0].wait()
    step = block_rows // SENDS
    sent = []
    for part in range(SENDS):
        span = slice(part * step, (part + 1) * step)
        for i in range(blocks):
            normed[part, i] = (layer_norm(points[i, span].astype(F32)) * norm_attn[...]).astype(BF16)
        for k, peer in enumerate(others):
            stage[part, k] = normed[part, block_for(dest, peer)]
        got[part][me] = normed[part, block_for(dest, me)]
        if part == 0:
            pl.semaphore_wait(barrier, len(partners))
        for k, peer in enumerate(others):
            sent.append(
                start_send(stage.at[part, k], got[part].at[me], send_sem.at[part, k], recv_sem.at[part, k],
                           at(peer))
            )
    for load in loads[1:]:
        load.wait()
    piece = block_rows // PARTS
    part_rows = blocks * piece
    for part in range(PARTS):
        for i in range(blocks):
            cot_parts[part, i * piece : (i + 1) * piece] = cot[
                i * block_rows + part * piece : i * block_rows + (part + 1) * piece
            ]
    w_hidden_t[...] = w_hidden[...].astype(F32).T.astype(BF16)
    w_output_t[...] = w_output[...].astype(F32).T.astype(BF16)
    for part in range(PARTS):
        dact[:, part * part_rows : (part + 1) * part_rows] = dot_rows(w_output[...], cot_parts[part])

    query_rows = PATCH_BLOCKS * piece
    pieces_sent = PARTS // SENDS
    for part in range(SENDS):
        for copy in sent[part * (peers - 1) : (part + 1) * (peers - 1)]:
            copy.wait_recv()
        for j in range(blocks):
            block = got[part][src[j]]
            for q in range(pieces_sent):
                start = j // PATCH_BLOCKS * patch + (part * pieces_sent + q) * query_rows + j % PATCH_BLOCKS * piece
                feats[start : start + piece] = block[q * piece : (q + 1) * piece]
        for first in range(0, rows, patch):
            these = slice(first + part * patch // SENDS, first + (part + 1) * patch // SENDS)
            qkv[these] = dot(feats[these], w_qkv[...]).astype(BF16)

    returned = []
    for part in range(PARTS):
        att[...] = jnp.zeros_like(att)
        for n in range(rows // patch):
            some_queries(qkv, att, n * patch, patch, n * patch + part * query_rows, query_rows, n * query_rows)
        packed[part] = att[...].astype(BF16).reshape(blocks, piece, D)
        for k, peer in enumerate(others):
            back_stage[part, k] = packed[part, block_for(src, peer)]
            returned.append(
                start_send(back_stage.at[part, k], back[part].at[me], back_send.at[part, k],
                           back_recv.at[part, k], at(peer))
            )
        back[part][me] = packed[part, block_for(src, me)]

    chunks = w_hidden_t.shape[0] // UNITS
    share = UNITS * peers // w_hidden_t.shape[0]
    units = UNITS // share
    pairs = share // 2
    quarter = 2 * units // xs
    pair, along_x = [], []

    def to_pair(chunk):
        for j in range(pairs):
            pair.append(
                start_send(terms.at[chunk * share + 2 * j + (1 - core)], pair_in.at[chunk * pairs + j],
                           pair_send.at[chunk * pairs + j], pair_recv.at[chunk * pairs + j], at(y * 2 + 1 - core))
            )

    def to_x(chunk):
        for j in range(pairs):
            pair[chunk * pairs + j].wait_recv()
            both = terms[chunk * share + 2 * j + core].astype(F32) + pair_in[chunk * pairs + j].astype(F32)
            both = both.astype(BF16)
            for t in range(xs):
                x_out[chunk, t, j] = both[t * quarter : (t + 1) * quarter]
        for k in range(1, xs):
            along_x.append(
                start_send(x_out.at[chunk, (x + k) % xs], x_in.at[chunk, k - 1], x_send.at[chunk, k - 1],
                           x_recv.at[chunk, k - 1], on_x((x + k) % xs))
            )

    for part in range(PARTS):
        for copy in returned[part * (peers - 1) : (part + 1) * (peers - 1)]:
            copy.wait_recv()
        mixed = jnp.concatenate([back[part][dest[i]] for i in range(blocks)], axis=0)
        before = jnp.concatenate([points[i, part * piece : (part + 1) * piece] for i in range(blocks)], axis=0)
        hidden = (before.astype(F32) + dot(mixed, w_out[...])).astype(BF16)
        second[...] = (layer_norm(hidden.astype(F32)) * norm_mlp[...]).astype(BF16)
        these = slice(part * part_rows, (part + 1) * part_rows)
        for chunk in range(chunks):
            span = slice(chunk * UNITS, (chunk + 1) * UNITS)
            act, slope = gelu_and_slope(dot_rows(w_hidden_t[span], second[...]))
            act = act.astype(BF16)
            dpre = (dact[span, these] * slope).astype(BF16)
            out_part, hid_part = dot(act, cot_parts[part]), dot(dpre, second[...])
            if part:
                out_part, hid_part = out_acc[span] + out_part, hid_acc[span] + hid_part
            if part < PARTS - 1:
                out_acc[span], hid_acc[span] = out_part, hid_part
            else:
                for j in range(share):
                    mine = slice(j * units, (j + 1) * units)
                    terms[chunk * share + j, :units] = hid_part[mine].astype(BF16)
                    terms[chunk * share + j, units:] = out_part[mine].astype(BF16)
                to_pair(chunk)
                if chunk:
                    to_x(chunk - 1)
            added = dot(w_output_t[:, span], act)
            result[...] = added if chunk == 0 else result[...] + added
        if part == PARTS - 1:
            to_x(chunks - 1)
        ended = (hidden.astype(F32) + result[...].T).astype(BF16)
        for i in range(blocks):
            answer[i, part * piece : (part + 1) * piece] = ended[i * piece : (i + 1) * piece]
    store = pltpu.make_async_copy(answer, out_any, out_sem)
    store.start()

    for copy in along_x:
        copy.wait_recv()
    for chunk in range(chunks):
        for j in range(pairs):
            mine = x_out[chunk, x, j].astype(F32)
            for k in range(xs - 1):
                mine = mine + x_in[chunk, k, j].astype(F32)
            y_out[chunk * pairs + j] = mine.astype(BF16)
    along_y = [
        start_send(y_out.at[(y + k) % ys], y_in.at[k - 1], y_send.at[k - 1], y_recv.at[k - 1],
                   at((y + k) % ys * 2 + core))
        for k in range(1, ys)
    ]
    mine = y_out[y].astype(F32)
    for k, copy in enumerate(along_y):
        copy.wait_recv()
        mine = mine + y_in[k].astype(F32)
    z_all[z] = mine.astype(BF16)
    along_z = [
        start_send(z_all.at[z], z_all.at[z], z_send.at[k - 1], z_recv.at[k - 1], on_z((z + k) % zs))
        for k in range(1, zs)
    ]
    for copy in along_z:
        copy.wait_recv()
    total = z_all[0].astype(F32)
    for k in range(1, zs):
        total = total + z_all[k].astype(F32)
    x_all[x] = total * scale
    last = [
        start_send(x_all.at[x], x_all.at[x], g_send.at[k - 1], g_recv.at[k - 1], on_x((x + k) % xs))
        for k in range(1, xs)
    ]
    for copy in last:
        copy.wait_recv()
    sums = x_all[...].reshape(2 * units, D)
    hidden_grad[...] = sums[:units]
    output_grad[...] = sums[units:]
    for copy in [*sent, *returned, *pair, *along_x, *along_y, *along_z, *last]:
        copy.wait_send()
    store.wait()


def per_device(
    points, cotangent, dest_code, src_code, w_qkv, w_out, norm_attn, norm_mlp, w_hidden, w_output
):
    peers, groups = lax.axis_size("peer"), lax.axis_size("group")
    xs = 4 if groups % 4 == 0 else 1
    ys, zs = peers // 2, groups // xs
    blocks, rows = dest_code.shape[0], points.shape[0]
    block_rows, ff = rows // blocks, w_output.shape[0]
    scale = float(1.0 / np.sqrt(np.float32(rows * peers * groups)))
    units = ff // peers
    chunks, pairs = ff // UNITS, UNITS // units // 2
    quarter = 2 * units // xs
    vmem, smem = pl.BlockSpec(memory_space=pltpu.VMEM), pl.BlockSpec(memory_space=pltpu.SMEM)
    far = pl.BlockSpec(memory_space=pl.ANY)
    dma = pltpu.SemaphoreType.DMA
    some = max(xs - 1, 1)
    held = lambda shape, dtype=BF16: pltpu.VMEM(shape, dtype)
    result, hidden_grad, output_grad = pl.pallas_call(
        functools.partial(block_kernel, peers, xs, zs, scale),
        out_shape=(
            jax.ShapeDtypeStruct((blocks, block_rows, D), BF16),
            jax.ShapeDtypeStruct((units, D), F32),
            jax.ShapeDtypeStruct((units, D), F32),
        ),
        in_specs=[far, far, smem, smem, far, far, vmem, vmem, far, far],
        out_specs=(far, vmem, vmem),
        scratch_shapes=[
            held((blocks, block_rows, D)), held((rows, D)), held((D, 3 * D)), held((D, D)),
            held((D, ff)), held((ff, D)), held((ff, D)), held((D, ff)),
            held((PARTS, rows // PARTS, D)),
            held((SENDS, blocks, block_rows // SENDS, D)),
            held((SENDS, peers - 1, block_rows // SENDS, D)),
            (held((peers, block_rows // SENDS, D)),) * SENDS,
            held((rows, D)), held((rows, 3 * D)), held((rows // PARTS, D), F32),
            held((PARTS, blocks, block_rows // PARTS, D)),
            held((PARTS, peers - 1, block_rows // PARTS, D)),
            (held((peers, block_rows // PARTS, D)),) * PARTS,
            held((rows // PARTS, D)),
            held((ff, rows), F32), held((D, rows // PARTS), F32), held((blocks, block_rows, D)),
            held((ff, D), F32), held((ff, D), F32),
            held((peers, 2 * units, D)), held((ys, 2 * units, D)),
            held((chunks, xs, pairs, quarter, D)), held((chunks, some, pairs, quarter, D)),
            held((ys, quarter, D)), held((ys - 1, quarter, D)),
            held((zs, quarter, D)), held((xs, quarter, D), F32),
            dma((6,)), dma((SENDS, peers - 1)), dma((SENDS, peers - 1)),
            dma((PARTS, peers - 1)), dma((PARTS, peers - 1)),
            dma((ys,)), dma((ys,)), dma((chunks, some)), dma((chunks, some)),
            dma((ys - 1,)), dma((ys - 1,)), dma((max(zs - 1, 1),)), dma((max(zs - 1, 1),)),
            dma((some,)), dma((some,)), dma(()),
        ],
        compiler_params=pltpu.CompilerParams(
            collective_id=0, has_side_effects=True, vmem_limit_bytes=56 << 20
        ),
        cost_estimate=pl.CostEstimate(flops=1 << 33, bytes_accessed=4 << 20, transcendentals=1 << 23),
    )(points.reshape(blocks, block_rows, D), cotangent, dest_code, src_code, w_qkv, w_out,
      norm_attn.reshape(1, D), norm_mlp.reshape(1, D), w_hidden, w_output)
    return result.reshape(rows, D), hidden_grad.T, output_grad


def solution(mesh):
    return jax.shard_map(
        per_device,
        mesh=mesh,
        in_specs=(
            P(("group", "peer"), None),
            P(("group", "peer"), None),
            P(("group", "peer")),
            P(("group", "peer")),
            P(),
            P(),
            P(),
            P(),
            P(),
            P(),
        ),
        out_specs=(P(("group", "peer"), None), P(None, "peer"), P("peer", None)),
        check_vma=False,
    )
```

time: 113 us -> 110 us (0.973)
  Pallas kernels: 108 us -> 105 us
    pallas_call x1, Pallas kernels: 108 us -> 105 us  [per_device(): pl.pallas_call(functools.partial(block_kernel, peers, xs, zs, scale), out...]
    pallas_call x1 -> x0, local copies, waits for them, and re-layouts: 1.62 us -> none  [per_device(): pl.pallas_call(functools.partial(block_kernel, peers, xs, zs, scale), out...]
    unnamed x4 -> x7, local copies, waits for them, and re-layouts: 2.53 us -> 3.4 us
where the time goes in v5:
time: 110 us
  Pallas kernels  105 us (95%)
  local copies, waits for them, and re-layouts  3.4 us (3%)
    pallas_call x1, Pallas kernels, per_device(): pl.pallas_call(functools.partial(block_kernel, peers, xs, zs, scale), out...  105 us
    unnamed x7, local copies, waits for them, and re-layouts  3.4 us

profile of v5, /device:TPU:1, one launch (start us, length us, event | category | flops | bytes accessed | tf_op | source)
XLA Modules:
  0.0 109.5 jit_solution(7615355961954673800)
XLA Ops:
  0.6 105.5 %shard_map.121 = (bf16[8,128,256]{2,1,0:T(8,128)(2,1)}, f32[64,256]{1,0:T(8,128)}, f32[64,256]{1,0:T(8,128)}) custom-call(bf16[8,128,256]{2,1,0:T(8,128)(2,1)} %bitcast.7, bf16[1024,256]{1,0:T(8,128)(2,1)} %cot_any.1, s32[8]{0:T(128)} %dest.1, s32[8]{0:T(128)} %src.1, bf16[256,768]{1,0:T(8,128)(2,1)} %w_qkv_any.1, bf16[256,256]{1,0:T(8,128)(2,1)} %w_out_any.1, ...), custom_call_target="tpu_custom_call" | custom-call | flops 8589934592 | bytes 4194304 | tf_op jit(solution)/shard_map/pallas_call | solution.py:309
  106.1 0.0 copy-start.1
  106.1 1.9 %copy.16 = bf16[1024,256]{1,0:T(8,128)(2,1)} copy(bf16[1024,256]{1,0:T(8,128)(2,1)} %bitcast.5) | data formatting | bytes 1048576
  108.0 0.0 copy-done.1
  108.0 0.0 copy-start
  108.0 0.6 copy.17
  108.7 0.2 copy-done
  108.9 0.6 copy.18
Async XLA Ops:
  106.1 1.9 %copy-start.1 = (f32[64,256]{1,0:T(8,128)S(1)}, f32[64,256]{1,0:T(8,128)}, u32[]{:S(2)}) copy-start(f32[64,256]{1,0:T(8,128)} %get-tuple-element.7) | copy-start | bytes 196612
  108.0 0.9 copy-start

commit v6 on v5

--- a/solution.py
+++ b/solution.py
@@ -188,8 +188,8 @@
     share = UNITS * peers // w_hidden_t.shape[0]
     units = UNITS // share
     pairs = share // 2
-    quarter = 2 * units // xs
-    pair, along_x = [], []
+    quarter = units // xs
+    pair, along_x = [], ([], [])
 
     def to_pair(chunk):
         for j in range(pairs):
@@ -198,17 +198,21 @@
                            pair_send.at[chunk * pairs + j], pair_recv.at[chunk * pairs + j], at(y * 2 + 1 - core))
             )
 
-    def to_x(chunk):
+    def to_x(chunk, half):
         for j in range(pairs):
-            pair[chunk * pairs + j].wait_recv()
-            both = terms[chunk * share + 2 * j + core].astype(F32) + pair_in[chunk * pairs + j].astype(F32)
-            both = both.astype(BF16)
+            if half == 0:
+                pair[chunk * pairs + j].wait_recv()
+            side = slice(half * units, (half + 1) * units)
+            both = (
+                terms[chunk * share + 2 * j + core, side].astype(F32)
+                + pair_in[chunk * pairs + j, side].astype(F32)
+            ).astype(BF16)
             for t in range(xs):
-                x_out[chunk, t, j] = both[t * quarter : (t + 1) * quarter]
+                x_out[half, chunk, t, j] = both[t * quarter : (t + 1) * quarter]
         for k in range(1, xs):
-            along_x.append(
-                start_send(x_out.at[chunk, (x + k) % xs], x_in.at[chunk, k - 1], x_send.at[chunk, k - 1],
-                           x_recv.at[chunk, k - 1], on_x((x + k) % xs))
+            along_x[half].append(
+                start_send(x_out.at[half, chunk, (x + k) % xs], x_in.at[half, chunk, k - 1],
+                           x_send.at[half, chunk, k - 1], x_recv.at[half, chunk, k - 1], on_x((x + k) % xs))
             )
 
     for part in range(PARTS):
@@ -236,55 +240,63 @@
                     terms[chunk * share + j, units:] = out_part[mine].astype(BF16)
                 to_pair(chunk)
                 if chunk:
-                    to_x(chunk - 1)
+                    to_x(chunk - 1, 0)
             added = dot(w_output_t[:, span], act)
             result[...] = added if chunk == 0 else result[...] + added
         if part == PARTS - 1:
-            to_x(chunks - 1)
+            to_x(chunks - 1, 0)
+            for chunk in range(chunks):
+                to_x(chunk, 1)
         ended = (hidden.astype(F32) + result[...].T).astype(BF16)
         for i in range(blocks):
             answer[i, part * piece : (part + 1) * piece] = ended[i * piece : (i + 1) * piece]
     store = pltpu.make_async_copy(answer, out_any, out_sem)
     store.start()
 
-    for copy in along_x:
-        copy.wait_recv()
-    for chunk in range(chunks):
-        for j in range(pairs):
-            mine = x_out[chunk, x, j].astype(F32)
-            for k in range(xs - 1):
-                mine = mine + x_in[chunk, k, j].astype(F32)
-            y_out[chunk * pairs + j] = mine.astype(BF16)
-    along_y = [
-        start_send(y_out.at[(y + k) % ys], y_in.at[k - 1], y_send.at[k - 1], y_recv.at[k - 1],
-                   at((y + k) % ys * 2 + core))
-        for k in range(1, ys)
-    ]
-    mine = y_out[y].astype(F32)
-    for k, copy in enumerate(along_y):
-        copy.wait_recv()
-        mine = mine + y_in[k].astype(F32)
-    z_all[z] = mine.astype(BF16)
-    along_z = [
-        start_send(z_all.at[z], z_all.at[z], z_send.at[k - 1], z_recv.at[k - 1], on_z((z + k) % zs))
-        for k in range(1, zs)
-    ]
-    for copy in along_z:
-        copy.wait_recv()
-    total = z_all[0].astype(F32)
-    for k in range(1, zs):
-        total = total + z_all[k].astype(F32)
-    x_all[x] = total * scale
-    last = [
-        start_send(x_all.at[x], x_all.at[x], g_send.at[k - 1], g_recv.at[k - 1], on_x((x + k) % xs))
-        for k in range(1, xs)
-    ]
-    for copy in last:
-        copy.wait_recv()
-    sums = x_all[...].reshape(2 * units, D)
-    hidden_grad[...] = sums[:units]
-    output_grad[...] = sums[units:]
-    for copy in [*sent, *returned, *pair, *along_x, *along_y, *along_z, *last]:
+    along_y, along_z, last = ([], []), ([], []), ([], [])
+    for half in range(2):
+        for copy in along_x[half]:
+            copy.wait_recv()
+        for chunk in range(chunks):
+            for j in range(pairs):
+                mine = x_out[half, chunk, x, j].astype(F32)
+                for k in range(xs - 1):
+                    mine = mine + x_in[half, chunk, k, j].astype(F32)
+                y_out[half, chunk * pairs + j] = mine.astype(BF16)
+        for k in range(1, ys):
+            along_y[half].append(
+                start_send(y_out.at[half, (y + k) % ys], y_in.at[half, k - 1], y_send.at[half, k - 1],
+                           y_recv.at[half, k - 1], at((y + k) % ys * 2 + core))
+            )
+    for half in range(2):
+        mine = y_out[half, y].astype(F32)
+        for k, copy in enumerate(along_y[half]):
+            copy.wait_recv()
+            mine = mine + y_in[half, k].astype(F32)
+        z_all[half, z] = mine.astype(BF16)
+        for k in range(1, zs):
+            along_z[half].append(
+                start_send(z_all.at[half, z], z_all.at[half, z], z_send.at[half, k - 1],
+                           z_recv.at[half, k - 1], on_z((z + k) % zs))
+            )
+    for half in range(2):
+        for copy in along_z[half]:
+            copy.wait_recv()
+        total = z_all[half, 0].astype(F32)
+        for k in range(1, zs):
+            total = total + z_all[half, k].astype(F32)
+        x_all[half, x] = total * scale
+        for k in range(1, xs):
+            last[half].append(
+                start_send(x_all.at[half, x], x_all.at[half, x], g_send.at[half, k - 1],
+                           g_recv.at[half, k - 1], on_x((x + k) % xs))
+            )
+    for half, grad in enumerate((hidden_grad, output_grad)):
+        for copy in last[half]:
+            copy.wait_recv()
+        grad[...] = x_all[half].reshape(units, D)
+    both = [copy for stage in (along_x, along_y, along_z, last) for half in stage for copy in half]
+    for copy in [*sent, *returned, *pair, *both]:
         copy.wait_send()
     store.wait()
 
@@ -300,7 +312,7 @@
     scale = float(1.0 / np.sqrt(np.float32(rows * peers * groups)))
     units = ff // peers
     chunks, pairs = ff // UNITS, UNITS // units // 2
-    quarter = 2 * units // xs
+    quarter = units // xs
     vmem, smem = pl.BlockSpec(memory_space=pltpu.VMEM), pl.BlockSpec(memory_space=pltpu.SMEM)
     far = pl.BlockSpec(memory_space=pl.ANY)
     dma = pltpu.SemaphoreType.DMA
@@ -330,14 +342,14 @@
             held((ff, rows), F32), held((D, rows // PARTS), F32), held((blocks, block_rows, D)),
             held((ff, D), F32), held((ff, D), F32),
             held((peers, 2 * units, D)), held((ys, 2 * units, D)),
-            held((chunks, xs, pairs, quarter, D)), held((chunks, some, pairs, quarter, D)),
-            held((ys, quarter, D)), held((ys - 1, quarter, D)),
-            held((zs, quarter, D)), held((xs, quarter, D), F32),
+            held((2, chunks, xs, pairs, quarter, D)), held((2, chunks, some, pairs, quarter, D)),
+            held((2, ys, quarter, D)), held((2, ys - 1, quarter, D)),
+            held((2, zs, quarter, D)), held((2, xs, quarter, D), F32),
             dma((6,)), dma((SENDS, peers - 1)), dma((SENDS, peers - 1)),
             dma((PARTS, peers - 1)), dma((PARTS, peers - 1)),
-            dma((ys,)), dma((ys,)), dma((chunks, some)), dma((chunks, some)),
-            dma((ys - 1,)), dma((ys - 1,)), dma((max(zs - 1, 1),)), dma((max(zs - 1, 1),)),
-            dma((some,)), dma((some,)), dma(()),
+            dma((ys,)), dma((ys,)), dma((2, chunks, some)), dma((2, chunks, some)),
+            dma((2, ys - 1)), dma((2, ys - 1)), dma((2, max(zs - 1, 1))), dma((2, max(zs - 1, 1))),
+            dma((2, some)), dma((2, some)), dma(()),
         ],
         compiler_params=pltpu.CompilerParams(
             collective_id=0, has_side_effects=True, vmem_limit_bytes=56 << 20

time: 110 us -> 107 us (0.973)
  Pallas kernels: 105 us -> 103 us
    pallas_call x1, Pallas kernels: 105 us -> 103 us  [per_device(): pl.pallas_call(functools.partial(block_kernel, peers, xs, zs, scale), out...]
where the time goes in v6:
time: 107 us
  Pallas kernels  103 us (96%)
  local copies, waits for them, and re-layouts  3.4 us (3%)
    pallas_call x1, Pallas kernels, per_device(): pl.pallas_call(functools.partial(block_kernel, peers, xs, zs, scale), out...  103 us
    unnamed x7, local copies, waits for them, and re-layouts  3.4 us

profile of v6, /device:TPU:1, one launch (start us, length us, event | category | flops | bytes accessed | tf_op | source)
XLA Modules:
  0.0 107.2 jit_solution(14780399541961099501)
XLA Ops:
  0.6 103.2 %shard_map.121 = (bf16[8,128,256]{2,1,0:T(8,128)(2,1)}, f32[64,256]{1,0:T(8,128)}, f32[64,256]{1,0:T(8,128)}) custom-call(bf16[8,128,256]{2,1,0:T(8,128)(2,1)} %bitcast.7, bf16[1024,256]{1,0:T(8,128)(2,1)} %cot_any.1, s32[8]{0:T(128)} %dest.1, s32[8]{0:T(128)} %src.1, bf16[256,768]{1,0:T(8,128)(2,1)} %w_qkv_any.1, bf16[256,256]{1,0:T(8,128)(2,1)} %w_out_any.1, ...), custom_call_target="tpu_custom_call" | custom-call | flops 8589934592 | bytes 4194304 | tf_op jit(solution)/shard_map/pallas_call | solution.py:321
  103.8 0.0 copy-start.1
  103.8 1.9 %copy.16 = bf16[1024,256]{1,0:T(8,128)(2,1)} copy(bf16[1024,256]{1,0:T(8,128)(2,1)} %bitcast.5) | data formatting | bytes 1048576
  105.7 0.0 copy-done.1
  105.7 0.0 copy-start
  105.7 0.6 copy.17
  106.3 0.2 copy-done
  106.6 0.6 copy.18
Async XLA Ops:
  103.8 1.9 %copy-start.1 = (f32[64,256]{1,0:T(8,128)S(1)}, f32[64,256]{1,0:T(8,128)}, u32[]{:S(2)}) copy-start(f32[64,256]{1,0:T(8,128)} %get-tuple-element.7) | copy-start | bytes 196612
  105.7 0.9 copy-start

commit v7 on v6

--- a/solution.py
+++ b/solution.py
@@ -49,6 +49,10 @@
     )
     copy.start()
     return copy
+
+
+def far_first(count):
+    return sorted(range(1, count), key=lambda k: -min(k, count - k))
 
 
 def block_for(codes, peer):
@@ -107,7 +111,7 @@
     blocks, block_rows = points.shape[0], points.shape[1]
     rows = blocks * block_rows
     patch = PATCH_BLOCKS * block_rows
-    others = [(me + k) % peers for k in range(1, peers)]
+    others = [(me + k) % peers for k in far_first(peers)]
 
     def at(peer):
         return {"group": group, "peer": peer}
@@ -209,7 +213,7 @@
             ).astype(BF16)
             for t in range(xs):
                 x_out[half, chunk, t, j] = both[t * quarter : (t + 1) * quarter]
-        for k in range(1, xs):
+        for k in far_first(xs):
             along_x[half].append(
                 start_send(x_out.at[half, chunk, (x + k) % xs], x_in.at[half, chunk, k - 1],
                            x_send.at[half, chunk, k - 1], x_recv.at[half, chunk, k - 1], on_x((x + k) % xs))
@@ -263,18 +267,19 @@
                 for k in range(xs - 1):
                     mine = mine + x_in[half, chunk, k, j].astype(F32)
                 y_out[half, chunk * pairs + j] = mine.astype(BF16)
-        for k in range(1, ys):
+        for k in far_first(ys):
             along_y[half].append(
                 start_send(y_out.at[half, (y + k) % ys], y_in.at[half, k - 1], y_send.at[half, k - 1],
                            y_recv.at[half, k - 1], at((y + k) % ys * 2 + core))
             )
     for half in range(2):
         mine = y_out[half, y].astype(F32)
-        for k, copy in enumerate(along_y[half]):
-            copy.wait_recv()
+        for copy in along_y[half]:
+            copy.wait_recv()
+        for k in range(ys - 1):
             mine = mine + y_in[half, k].astype(F32)
         z_all[half, z] = mine.astype(BF16)
-        for k in range(1, zs):
+        for k in far_first(zs):
             along_z[half].append(
                 start_send(z_all.at[half, z], z_all.at[half, z], z_send.at[half, k - 1],
                            z_recv.at[half, k - 1], on_z((z + k) % zs))
@@ -286,7 +291,7 @@
         for k in range(1, zs):
             total = total + z_all[half, k].astype(F32)
         x_all[half, x] = total * scale
-        for k in range(1, xs):
+        for k in far_first(xs):
             last[half].append(
                 start_send(x_all.at[half, x], x_all.at[half, x], g_send.at[half, k - 1],
                            g_recv.at[half, k - 1], on_x((x + k) % xs))

time: 107 us -> 105 us (0.981); the launches traced: 107 us -> 104 us
  Pallas kernels: 103 us -> 99.6 us
    pallas_call x1, Pallas kernels: 103 us -> 99.6 us  [per_device(): pl.pallas_call(functools.partial(block_kernel, peers, xs, zs, scale), out...]
where the time goes in v7:
time: 105 us; the launch traced here: 104 us
  Pallas kernels  99.6 us (95%)
  local copies, waits for them, and re-layouts  3.4 us (3%)
    pallas_call x1, Pallas kernels, per_device(): pl.pallas_call(functools.partial(block_kernel, peers, xs, zs, scale), out...  99.6 us
    unnamed x7, local copies, waits for them, and re-layouts  3.4 us

profile of v7, /device:TPU:1, one launch (start us, length us, event | category | flops | bytes accessed | tf_op | source)
XLA Modules:
  0.0 103.6 jit_solution(13708030760316957329)
XLA Ops:
  0.6 99.6 %shard_map.121 = (bf16[8,128,256]{2,1,0:T(8,128)(2,1)}, f32[64,256]{1,0:T(8,128)}, f32[64,256]{1,0:T(8,128)}) custom-call(bf16[8,128,256]{2,1,0:T(8,128)(2,1)} %bitcast.7, bf16[1024,256]{1,0:T(8,128)(2,1)} %cot_any.1, s32[8]{0:T(128)} %dest.1, s32[8]{0:T(128)} %src.1, bf16[256,768]{1,0:T(8,128)(2,1)} %w_qkv_any.1, bf16[256,256]{1,0:T(8,128)(2,1)} %w_out_any.1, ...), custom_call_target="tpu_custom_call" | custom-call | flops 8589934592 | bytes 4194304 | tf_op jit(solution)/shard_map/pallas_call | solution.py:326
  100.2 0.0 copy-start.1
  100.2 1.9 %copy.16 = bf16[1024,256]{1,0:T(8,128)(2,1)} copy(bf16[1024,256]{1,0:T(8,128)(2,1)} %bitcast.5) | data formatting | bytes 1048576
  102.1 0.0 copy-done.1
  102.1 0.0 copy-start
  102.1 0.6 copy.17
  102.8 0.2 copy-done
  103.0 0.6 copy.18
Async XLA Ops:
  100.2 1.9 %copy-start.1 = (f32[64,256]{1,0:T(8,128)S(1)}, f32[64,256]{1,0:T(8,128)}, u32[]{:S(2)}) copy-start(f32[64,256]{1,0:T(8,128)} %get-tuple-element.7) | copy-start | bytes 196612
  102.1 0.9 copy-start
